TPU v7x, 32 devices: a whole 2x2x4 slice. The times are simulated.
32 devices in a mesh: wa: 8 (over z, x), sa: 4 (over y, core).
Axes of the slice: x: 2, y: 2, z: 4, core: 2. Of those that a mesh axis runs over, the one named last changes fastest.
Arguments:
- unit_entry_lines: bfloat16 [4096, 1024], P(('wa', 'sa')), may hold values from -6 to 6
- opening_stratum_contents: bfloat16 [4096, 1024], P(('wa', 'sa')), may hold values from -6 to 6
- packed_sequence_ids: int32 [4096], P(('wa', 'sa')), may hold values from 0 to 15, never falling along the last dimension, each value on 1 to 512 neighbouring positions
- unit_exit_slope: bfloat16 [4096, 1024], P(('wa', 'sa')), may hold values from -6 to 6
- earlier_norming_amplitude_arg: bfloat16 [1024], P('wa'), may hold values from 0.5 to 1.5
- earlier_norming_offset_arg: bfloat16 [1024], P('wa'), may hold values from -1.5 to 1.5
- token_lag_blends: bfloat16 [6144], P('wa'), may hold values from 0 to 1
- acceptor_mapping: bfloat16 [1048576], P('wa'), may hold values from -0.1875 to 0.1875
- lookup_mapping: bfloat16 [1048576], P('wa'), may hold values from -0.1875 to 0.1875
- content_mapping: bfloat16 [1048576], P('wa'), may hold values from -0.1875 to 0.1875
- exit_mapping: bfloat16 [1048576], P('wa'), may hold values from -0.375 to 0.375
- fading_feature_odds: bfloat16 [1024], P('wa'), may hold values from -12 to 2
- fading_leftside_array: bfloat16 [65536], P('wa'), may hold values from -0.1875 to 0.1875
- fading_rightside_array: bfloat16 [65536], P('wa'), may hold values from -0.375 to 0.375
- learning_speed_odds: bfloat16 [1024], P('wa'), may hold values from -4 to 4
- speed_leftside_array: bfloat16 [65536], P('wa'), may hold values from -0.1875 to 0.1875
- speed_rightside_array: bfloat16 [65536], P('wa'), may hold values from -0.75 to 0.75
- content_skip_odds: bfloat16 [1024], P('wa'), may hold values from -4 to 4
- content_skip_leftside: bfloat16 [32768], P('wa'), may hold values from -0.1875 to 0.1875
- content_skip_rightside: bfloat16 [32768], P('wa'), may hold values from -1 to 1
- valve_leftside_array: bfloat16 [163840], P('wa'), may hold values from -0.1875 to 0.1875
- valve_rightside_array: bfloat16 [163840], P('wa'), may hold values from -0.5 to 0.5
- erasure_lookup_stretch: bfloat16 [1024], P('wa'), may hold values from 0.29882812 to 1.5
- stored_lookup_speed: bfloat16 [1024], P('wa'), may hold values from 0.19921875 to 1.796875
- present_token_boost: bfloat16 [1024], P('wa'), may hold values from -3 to 3
- cluster_norming_amplitude_array: bfloat16 [1024], P('wa'), may hold values from 0.5 to 1.5
- cluster_norming_offset_array: bfloat16 [1024], P('wa'), may hold values from -1.5 to 1.5
- later_norming_amplitude_arg: bfloat16 [1024], P('wa'), may hold values from 0.5 to 1.5
- later_norming_offset_arg: bfloat16 [1024], P('wa'), may hold values from -1.5 to 1.5
- feature_lag_blend: bfloat16 [1024], P('wa'), may hold values from 0 to 1
- perceptron_lookup_array: bfloat16 [4194304], P('wa'), may hold values from -0.1875 to 0.1875
- perceptron_content_array: bfloat16 [4194304], P('wa'), may hold values from -0.09375 to 0.09375
Outputs:
- block_out: bfloat16 [4096, 1024], P(('wa', 'sa'))
- grad_block_in: float32 [4096, 1024], P(('wa', 'sa'))
- grad_value_first: float32 [4096, 1024], P(('wa', 'sa'))
- grad_ln1_gain: float32 [1024], P('wa')
- grad_ln1_bias: float32 [1024], P('wa')
- grad_mix_time: float32 [6144], P('wa')
- grad_w_receptance: float32 [1048576], P('wa')
- grad_w_key: float32 [1048576], P('wa')
- grad_w_value: float32 [1048576], P('wa')
- grad_w_output: float32 [1048576], P('wa')
- grad_decay_base: float32 [1024], P('wa')
- grad_decay_down: float32 [65536], P('wa')
- decay_second_factor_gradient: float32 [65536], P('wa')
- grad_rate_base: float32 [1024], P('wa')
- grad_rate_down: float32 [65536], P('wa')
- rate_second_factor_gradient: float32 [65536], P('wa')
- value_residual_logits_gradient: float32 [1024], P('wa')
- value_residual_first_gradient: float32 [32768], P('wa')
- value_residual_second_gradient: float32 [32768], P('wa')
- grad_gate_down: float32 [163840], P('wa')
- grad_gate_up: float32 [163840], P('wa')
- grad_key_norm: float32 [1024], P('wa')
- grad_key_rate: float32 [1024], P('wa')
- present_token_boost_slope: float32 [1024], P('wa')
- grad_lnx_gain: float32 [1024], P('wa')
- grad_lnx_bias: float32 [1024], P('wa')
- grad_ln2_gain: float32 [1024], P('wa')
- grad_ln2_bias: float32 [1024], P('wa')
- grad_mix_channel: float32 [1024], P('wa')
- grad_ffn_key: float32 [4194304], P('wa')
- grad_ffn_value: float32 [4194304], P('wa')
Inputs may be any that keep to these rules, and one draw needn't show every extreme that they name: `packed_sequence_ids`: segment numbers never fall along the tokens; a segment holds 1 to 512 tokens and may run over a sequence's start.
All inputs are finite; a program needn't handle non-finite values.
Results may differ from a plain program's by a relative error of at most 0.015.
The roundings to bfloat16 on the way count: a program that leaves them out, or rounds other values in their place, can miss the bound.
Values may be sent and summed in bfloat16 or wider, within the bound.
A program may use at most 256 MiB of HBM per device.

v0:
```python
import math

import jax
import jax.numpy as jnp
from jax import lax
from jax.sharding import PartitionSpec as P

NETWORK_WIDTH = 1024
HEAD_SIZE = 64
FEEDFORWARD_UNITS = 4096
DECAY_INNER = 64
RATE_INNER = 64
VALUE_RES_INNER = 32
GATE_INNER = 160


HIGHEST = lax.Precision.HIGHEST
DECAY_FACTOR = 0.606531
CLUSTER_EPSILON = 0.00064
NORM_EPS = 1e-05


def shifted_2(block, axis, distance):
    devices = range(lax.axis_size(axis))
    route = [(i - distance, i) for i in devices if i - distance in devices]
    return lax.ppermute(block, axis, route)


def entering(value, axis, combine, identity, reverse):
    devices, mine = (lax.axis_size(axis), lax.axis_index(axis))
    everything = jax.tree.map(
        lambda part, kind: lax.all_gather(part.astype(kind), axis),
        value,
        (jnp.bfloat16, jnp.bfloat16),
    )
    start = jax.tree.map(
        lambda part, zero: jnp.broadcast_to(jnp.asarray(zero, part.dtype), part.shape),
        value,
        identity,
    )

    def hop(k, before):
        at = devices - 1 - k if reverse else k
        reached = at > mine if reverse else at < mine
        new = combine(
            before, jax.tree.map(lambda part, own: part[at].astype(own.dtype), everything, value)
        )
        return jax.tree.map(lambda a, b: jnp.where(reached, a, b), new, before)

    return lax.fori_loop(0, devices, hop, start)


def shortened(value):

    def short(part):
        return part.astype(jnp.bfloat16) if part.dtype == jnp.float32 else part

    return jax.tree.map(short, value)


def layout():
    return (
        (NETWORK_WIDTH,),
        (NETWORK_WIDTH,),
        (6, NETWORK_WIDTH),
        (NETWORK_WIDTH, NETWORK_WIDTH),
        (NETWORK_WIDTH, NETWORK_WIDTH),
        (NETWORK_WIDTH, NETWORK_WIDTH),
        (NETWORK_WIDTH, NETWORK_WIDTH),
        (NETWORK_WIDTH,),
        (NETWORK_WIDTH, DECAY_INNER),
        (DECAY_INNER, NETWORK_WIDTH),
        (NETWORK_WIDTH,),
        (NETWORK_WIDTH, RATE_INNER),
        (RATE_INNER, NETWORK_WIDTH),
        (NETWORK_WIDTH,),
        (NETWORK_WIDTH, VALUE_RES_INNER),
        (VALUE_RES_INNER, NETWORK_WIDTH),
        (NETWORK_WIDTH, GATE_INNER),
        (GATE_INNER, NETWORK_WIDTH),
        (NETWORK_WIDTH,),
        (NETWORK_WIDTH,),
        (NETWORK_WIDTH,),
        (NETWORK_WIDTH,),
        (NETWORK_WIDTH,),
        (NETWORK_WIDTH,),
        (NETWORK_WIDTH,),
        (NETWORK_WIDTH,),
        (NETWORK_WIDTH, FEEDFORWARD_UNITS),
        (FEEDFORWARD_UNITS, NETWORK_WIDTH),
    )


def shaped(flat_parts):
    return tuple(
        (tensor_entry.reshape(target) for tensor_entry, target in zip(flat_parts, layout()))
    )


def matrices(tensor_bundle):
    return tuple(
        (tensor_bundle[number] for number in (3, 4, 5, 6, 8, 9, 11, 12, 14, 15, 16, 17, 26, 27))
    )


def layer_norm(values, scale_gain, shift_bias):
    average_level = values - jnp.mean(values, axis=1, keepdims=True)
    variance_width = jnp.mean(average_level * average_level, axis=1, keepdims=True)
    return average_level * lax.rsqrt(variance_width + NORM_EPS) * scale_gain + shift_bias


def prev_rows(values, edge_row, keeping):
    return jnp.concatenate([edge_row, values[:-1]], axis=0) * keeping[:, None]


def spread_mix(standardized_lines, before, mixing):
    delta = before - standardized_lines
    return tuple((standardized_lines + delta * mixing[number] for number in range(6)))


def channel_in(standardized_lines, before, mixing):
    return standardized_lines + (before - standardized_lines) * mixing


def prepare_inputs(
    acceptor_lines,
    key_projected_rows,
    unmixed_value_rows,
    decay_lowrank_output,
    value_residual_lowrank,
    rate_lowrank_output,
    initial_layer_value,
    fading_feature_odds,
    learning_speed_odds,
    content_skip_odds,
    erasure_lookup_stretch,
    stored_lookup_speed,
):
    decay_factors = jnp.exp(
        -DECAY_FACTOR * jax.nn.sigmoid(fading_feature_odds + decay_lowrank_output)
    )
    content_outcome_lines = unmixed_value_rows + (
        initial_layer_value - unmixed_value_rows
    ) * jax.nn.sigmoid(content_skip_odds + value_residual_lowrank)
    rate_sigmoid_gate = jax.nn.sigmoid(learning_speed_odds + rate_lowrank_output)
    head_shape = (acceptor_lines.shape[0], acceptor_lines.shape[1] // HEAD_SIZE, HEAD_SIZE)
    standardized_lines = (key_projected_rows * erasure_lookup_stretch).reshape(head_shape)
    standardized_lines = standardized_lines * lax.rsqrt(
        jnp.sum(standardized_lines * standardized_lines, axis=2, keepdims=True) + 1e-06
    )
    lagged_lookup_entry = key_projected_rows * (
        1.0 + (rate_sigmoid_gate - 1.0) * stored_lookup_speed
    )
    removal = standardized_lines * rate_sigmoid_gate.reshape(head_shape)
    return (
        acceptor_lines.reshape(head_shape),
        decay_factors.reshape(head_shape),
        lagged_lookup_entry.reshape(head_shape),
        content_outcome_lines.reshape(head_shape),
        standardized_lines,
        removal,
    )


def complete_unit(
    unit_outcomes,
    acceptor_lines,
    lagged_lookup_entry,
    content_outcome_lines,
    valve_exit_lines,
    cluster_norming_amplitude_lines,
    cluster_norming_offset_lines,
    present_token_boost,
):
    average_level = unit_outcomes - jnp.mean(unit_outcomes, axis=2, keepdims=True)
    variance_width = jnp.mean(average_level * average_level, axis=2, keepdims=True)
    linear_extent = (unit_outcomes.shape[0], unit_outcomes.shape[1] * unit_outcomes.shape[2])
    standardized_lines = (average_level * lax.rsqrt(variance_width + CLUSTER_EPSILON)).reshape(
        linear_extent
    ) * cluster_norming_amplitude_lines + cluster_norming_offset_lines
    boost_summed = jnp.sum(
        acceptor_lines * lagged_lookup_entry * present_token_boost.reshape(unit_outcomes.shape[1:]),
        axis=2,
        keepdims=True,
    )
    return (
        standardized_lines + (boost_summed * content_outcome_lines).reshape(linear_extent)
    ) * valve_exit_lines


def state_step(current, inputs):
    (
        acceptor_lines,
        decay_factors,
        keyed,
        content_outcome_lines,
        standardized_lines,
        removal,
        keeping,
    ) = inputs
    current = current * keeping
    current = (
        current * decay_factors[:, None, :]
        - jnp.sum(current * standardized_lines[:, None, :], axis=2, keepdims=True)
        * removal[:, None, :]
        + content_outcome_lines[:, :, None] * keyed[:, None, :]
    )
    return (current, jnp.sum(current * acceptor_lines[:, None, :], axis=2))


def sweep_block(current, block_inputs):
    return lax.scan(state_step, current, block_inputs)


def recurrence(initial, inputs, keeping):
    length = keeping.shape[0]
    block_size = math.gcd(length, 4)
    blocks = length // block_size
    folded = tuple(
        (
            tensor_entry.reshape((blocks, block_size) + tensor_entry.shape[1:])
            for tensor_entry in inputs + (keeping,)
        )
    )
    last_state, unit_outcomes = lax.scan(jax.checkpoint(sweep_block), initial, folded)
    return (unit_outcomes.reshape((length,) + unit_outcomes.shape[2:]), last_state)


def pair_step(carry, inputs):
    transit, current = carry
    (
        acceptor_lines,
        decay_factors,
        keyed,
        content_outcome_lines,
        standardized_lines,
        removal,
        keeping,
    ) = inputs
    transit = transit * keeping
    current = current * keeping
    transit = (
        transit * decay_factors[:, None, :]
        - jnp.sum(transit * standardized_lines[:, None, :], axis=2, keepdims=True)
        * removal[:, None, :]
    )
    current = (
        current * decay_factors[:, None, :]
        - jnp.sum(current * standardized_lines[:, None, :], axis=2, keepdims=True)
        * removal[:, None, :]
        + content_outcome_lines[:, :, None] * keyed[:, None, :]
    )
    return (
        (transit, current),
        (
            jnp.sum(current * acceptor_lines[:, None, :], axis=2),
            jnp.sum(transit * acceptor_lines[:, None, :], axis=2),
        ),
    )


def span_sweep(inputs, keep_span):
    head_count = inputs[0].shape[1]
    identity = jnp.broadcast_to(
        jnp.eye(HEAD_SIZE, dtype=jnp.float32), (head_count, HEAD_SIZE, HEAD_SIZE)
    )
    zero_state = jnp.zeros((head_count, HEAD_SIZE, HEAD_SIZE), jnp.float32)
    (span_map, span_shift), (local_out, carried) = lax.scan(
        pair_step, (identity, zero_state), inputs + (keep_span,)
    )
    return (span_map, span_shift, local_out, carried)


def span_back(initial, inputs, keep_span, grad_span, end_grad):

    def run_span(start, *members):
        return recurrence(start, members, keep_span)

    unused, pullback = jax.vjp(run_span, initial, *inputs)
    return pullback((grad_span, end_grad))[1:]


def chain_join(earlier, later):
    first_map, first_shift = earlier
    second_map, second_shift = later
    joined = jnp.einsum("hij,hjk->hik", first_map, second_map, precision=HIGHEST)
    shifted = jnp.einsum("hij,hjk->hik", first_shift, second_map, precision=HIGHEST) + second_shift
    return (joined, shifted)


def prefix_step(carry, tensor_entry):
    return (chain_join(carry, tensor_entry), carry)


def back_step(end_grad, tensor_entry):
    span_map, span_grad = tensor_entry
    start_grad = span_grad + jnp.einsum("hij,hlj->hil", end_grad, span_map, precision=HIGHEST)
    return (start_grad, end_grad)


def matrix_multiply(left, right):
    return jnp.dot(left, right, preferred_element_type=jnp.float32)


def matrix_product_pullback(grad_out, left_low, right):
    grad_low = grad_out.astype(jnp.bfloat16)
    grad_weight = lax.dot_general(
        left_low, grad_low, (((0,), (0,)), ((), ())), preferred_element_type=jnp.float32
    )
    grad_left = lax.dot_general(
        grad_low, right, (((1,), (1,)), ((), ())), preferred_element_type=jnp.float32
    )
    return (grad_left, grad_weight)


def body(
    unit_entry_lines,
    opening_stratum_contents,
    packed_sequence_ids,
    unit_exit_slope,
    earlier_norming_amplitude_arg,
    earlier_norming_offset_arg,
    token_lag_blends,
    acceptor_mapping,
    lookup_mapping,
    content_mapping,
    exit_mapping,
    fading_feature_odds,
    fading_leftside_array,
    fading_rightside_array,
    learning_speed_odds,
    speed_leftside_array,
    speed_rightside_array,
    content_skip_odds,
    content_skip_leftside,
    content_skip_rightside,
    valve_leftside_array,
    valve_rightside_array,
    erasure_lookup_stretch,
    stored_lookup_speed,
    present_token_boost,
    cluster_norming_amplitude_array,
    cluster_norming_offset_array,
    later_norming_amplitude_arg,
    later_norming_offset_arg,
    feature_lag_blend,
    perceptron_lookup_array,
    perceptron_content_array,
):
    shards = (
        earlier_norming_amplitude_arg,
        earlier_norming_offset_arg,
        token_lag_blends,
        acceptor_mapping,
        lookup_mapping,
        content_mapping,
        exit_mapping,
        fading_feature_odds,
        fading_leftside_array,
        fading_rightside_array,
        learning_speed_odds,
        speed_leftside_array,
        speed_rightside_array,
        content_skip_odds,
        content_skip_leftside,
        content_skip_rightside,
        valve_leftside_array,
        valve_rightside_array,
        erasure_lookup_stretch,
        stored_lookup_speed,
        present_token_boost,
        cluster_norming_amplitude_array,
        cluster_norming_offset_array,
        later_norming_amplitude_arg,
        later_norming_offset_arg,
        feature_lag_blend,
        perceptron_lookup_array,
        perceptron_content_array,
    )
    gathered = (
        lax.all_gather(shards[0], "wa", axis=0, tiled=True),
        lax.all_gather(shards[1], "wa", axis=0, tiled=True),
        lax.all_gather(shards[2], "wa", axis=0, tiled=True),
        lax.all_gather(shards[3], "wa", axis=0, tiled=True),
        lax.all_gather(shards[4], "wa", axis=0, tiled=True),
        lax.all_gather(shards[5], "wa", axis=0, tiled=True),
        lax.all_gather(shards[6], "wa", axis=0, tiled=True),
        lax.all_gather(shards[7], "wa", axis=0, tiled=True),
        lax.all_gather(shards[8], "wa", axis=0, tiled=True),
        lax.all_gather(shards[9], "wa", axis=0, tiled=True),
        lax.all_gather(shards[10], "wa", axis=0, tiled=True),
        lax.all_gather(shards[11], "wa", axis=0, tiled=True),
        lax.all_gather(shards[12], "wa", axis=0, tiled=True),
        lax.all_gather(shards[13], "wa", axis=0, tiled=True),
        lax.all_gather(shards[14], "wa", axis=0, tiled=True),
        lax.all_gather(shards[15], "wa", axis=0, tiled=True),
        lax.all_gather(shards[16], "wa", axis=0, tiled=True),
        lax.all_gather(shards[17], "wa", axis=0, tiled=True),
        lax.all_gather(shards[18], "wa", axis=0, tiled=True),
        lax.all_gather(shards[19], "wa", axis=0, tiled=True),
        lax.all_gather(shards[20], "wa", axis=0, tiled=True),
        lax.all_gather(shards[21], "wa", axis=0, tiled=True),
        lax.all_gather(shards[22], "wa", axis=0, tiled=True),
        lax.all_gather(shards[23], "wa", axis=0, tiled=True),
        lax.all_gather(shards[24], "wa", axis=0, tiled=True),
        lax.all_gather(shards[25], "wa", axis=0, tiled=True),
        lax.all_gather(shards[26], "wa", axis=0, tiled=True),
        lax.all_gather(shards[27], "wa", axis=0, tiled=True),
    )
    tensor_bundle = shaped(gathered)
    small = [
        tensor_bundle[number].astype(jnp.float32)
        for number in (0, 1, 2, 7, 10, 13, 18, 19, 20, 21, 22, 23, 24, 25)
    ]
    (
        earlier_norming_amplitude,
        earlier_norming_offset,
        lagged_blend_lines,
        fading_odds_offset,
        speed_odds_offset,
        content_skip_odds_offset,
        unitnorm_erasure_lookup,
        speed_weighted_lookup,
        boost_blend,
        cluster_norming_amplitude_arg,
        cluster_norming_offset_arg,
        later_norming_amplitude,
        later_norming_offset,
        feature_blend_lines,
    ) = small
    (
        acceptor_array_formed,
        lookup_array_formed,
        content_array_formed,
        exit_array_formed,
        fading_narrow_array,
        fading_widen_array,
        speed_narrow_array,
        speed_widen_array,
        content_skip_narrow_array,
        content_skip_widen_array,
        valve_narrow_array,
        valve_widen_array,
        latent_entry_array,
        latent_exit_array,
    ) = matrices(tensor_bundle)
    length = unit_entry_lines.shape[0]
    model_width = unit_entry_lines.shape[1]
    residual_in = unit_entry_lines.astype(jnp.float32)
    initial_layer_value = opening_stratum_contents.astype(jnp.float32)
    normed_one, ln_one_back = jax.vjp(
        layer_norm, residual_in, earlier_norming_amplitude, earlier_norming_offset
    )
    edge_one, edge_segment = shifted_2(
        (normed_one[-1:], packed_sequence_ids[-1:].astype(jnp.float32)), "sa", 1
    )
    first_fresh = jnp.where(
        lax.axis_index("sa") == 0,
        1.0,
        jnp.where(packed_sequence_ids[0].astype(jnp.float32) != edge_segment[0], 1.0, 0.0),
    )
    fresh_rows = jnp.concatenate(
        [
            first_fresh[None].astype(jnp.float32),
            jnp.where(packed_sequence_ids[1:] != packed_sequence_ids[:-1], 1.0, 0.0).astype(
                jnp.float32
            ),
        ]
    )
    keeping = 1.0 - fresh_rows

    def shift_rows(row_block, edge_row):
        return prev_rows(row_block, edge_row, keeping)

    before_one, prev_one_back = jax.vjp(shift_rows, normed_one, edge_one)
    mixed, mix_back = jax.vjp(spread_mix, normed_one, before_one, lagged_blend_lines)
    recept_in, decay_input_rows, key_in, value_input_rows, rate_input_rows, gate_in = tuple(
        (tensor_entry.astype(jnp.bfloat16) for tensor_entry in mixed)
    )
    acceptor_lines = matrix_multiply(recept_in, acceptor_array_formed)
    key_projected_rows = matrix_multiply(key_in, lookup_array_formed)
    unmixed_value_rows = matrix_multiply(value_input_rows, content_array_formed)
    decay_hidden = jnp.tanh(matrix_multiply(decay_input_rows, fading_narrow_array))
    decay_lowrank_hidden = decay_hidden.astype(jnp.bfloat16)
    decay_lowrank_output = matrix_multiply(decay_lowrank_hidden, fading_widen_array)
    rate_hidden_rows = matrix_multiply(rate_input_rows, speed_narrow_array).astype(jnp.bfloat16)
    rate_lowrank_output = matrix_multiply(rate_hidden_rows, speed_widen_array)
    value_residual_hidden = matrix_multiply(value_input_rows, content_skip_narrow_array).astype(
        jnp.bfloat16
    )
    value_residual_lowrank = matrix_multiply(value_residual_hidden, content_skip_widen_array)
    gate_sig = jax.nn.sigmoid(matrix_multiply(gate_in, valve_narrow_array))
    gate_low = gate_sig.astype(jnp.bfloat16)
    valve_exit_lines = matrix_multiply(gate_low, valve_widen_array)
    readied_arguments, prepare_back = jax.vjp(
        prepare_inputs,
        acceptor_lines,
        key_projected_rows,
        unmixed_value_rows,
        decay_lowrank_output,
        value_residual_lowrank,
        rate_lowrank_output,
        initial_layer_value,
        fading_odds_offset,
        speed_odds_offset,
        content_skip_odds_offset,
        unitnorm_erasure_lookup,
        speed_weighted_lookup,
    )
    head_count = model_width // HEAD_SIZE
    identity = jnp.broadcast_to(
        jnp.eye(HEAD_SIZE, dtype=jnp.float32), (head_count, HEAD_SIZE, HEAD_SIZE)
    )
    zero_state = jnp.zeros((head_count, HEAD_SIZE, HEAD_SIZE), jnp.float32)
    block_len = math.gcd(length, 32)
    block_count = length // block_len

    def fold(tensor_entry):
        return tensor_entry.reshape((block_count, block_len) + tensor_entry.shape[1:])

    folded = tuple((fold(tensor_entry) for tensor_entry in readied_arguments))
    keep_folded = fold(keeping)
    span_maps, span_shifts, local_out, carried = jax.vmap(span_sweep)(folded, keep_folded)
    (block_map, block_shift), (start_map, start_shift) = lax.scan(
        prefix_step, (identity, zero_state), (span_maps, span_shifts)
    )
    prior_map, prior_state = entering(
        (block_map, block_shift), "sa", chain_join, (identity, zero_state), False
    )
    start_states = (
        jnp.einsum("hij,khjl->khil", prior_state, start_map, precision=HIGHEST) + start_shift
    )
    unit_outcomes = (
        local_out + jnp.einsum("khij,klhj->klhi", start_states, carried, precision=HIGHEST)
    ).reshape((length, head_count, HEAD_SIZE))
    blended_outcome, finish_back = jax.vjp(
        complete_unit,
        unit_outcomes,
        readied_arguments[0],
        readied_arguments[2],
        readied_arguments[3],
        valve_exit_lines,
        cluster_norming_amplitude_arg,
        cluster_norming_offset_arg,
        boost_blend,
    )
    mixed_low = blended_outcome.astype(jnp.bfloat16)
    residual_mid = residual_in + matrix_multiply(mixed_low, exit_array_formed)
    normed_two, ln_two_back = jax.vjp(
        layer_norm, residual_mid, later_norming_amplitude, later_norming_offset
    )
    edge_two = shifted_2(normed_two[-1:], "sa", 1)
    before_two, prev_two_back = jax.vjp(shift_rows, normed_two, edge_two)
    channel, chan_back = jax.vjp(channel_in, normed_two, before_two, feature_blend_lines)
    channel_low = channel.astype(jnp.bfloat16)
    pre_act = matrix_multiply(channel_low, latent_entry_array)
    hidden_low = jnp.square(jax.nn.relu(pre_act)).astype(jnp.bfloat16)
    block_out = residual_mid + matrix_multiply(hidden_low, latent_exit_array)
    regathered = (
        lax.all_gather(shards[0], "wa", axis=0, tiled=True),
        lax.all_gather(shards[1], "wa", axis=0, tiled=True),
        lax.all_gather(shards[2], "wa", axis=0, tiled=True),
        lax.all_gather(shards[3], "wa", axis=0, tiled=True),
        lax.all_gather(shards[4], "wa", axis=0, tiled=True),
        lax.all_gather(shards[5], "wa", axis=0, tiled=True),
        lax.all_gather(shards[6], "wa", axis=0, tiled=True),
        lax.all_gather(shards[7], "wa", axis=0, tiled=True),
        lax.all_gather(shards[8], "wa", axis=0, tiled=True),
        lax.all_gather(shards[9], "wa", axis=0, tiled=True),
        lax.all_gather(shards[10], "wa", axis=0, tiled=True),
        lax.all_gather(shards[11], "wa", axis=0, tiled=True),
        lax.all_gather(shards[12], "wa", axis=0, tiled=True),
        lax.all_gather(shards[13], "wa", axis=0, tiled=True),
        lax.all_gather(shards[14], "wa", axis=0, tiled=True),
        lax.all_gather(shards[15], "wa", axis=0, tiled=True),
        lax.all_gather(shards[16], "wa", axis=0, tiled=True),
        lax.all_gather(shards[17], "wa", axis=0, tiled=True),
        lax.all_gather(shards[18], "wa", axis=0, tiled=True),
        lax.all_gather(shards[19], "wa", axis=0, tiled=True),
        lax.all_gather(shards[20], "wa", axis=0, tiled=True),
        lax.all_gather(shards[21], "wa", axis=0, tiled=True),
        lax.all_gather(shards[22], "wa", axis=0, tiled=True),
        lax.all_gather(shards[23], "wa", axis=0, tiled=True),
        lax.all_gather(shards[24], "wa", axis=0, tiled=True),
        lax.all_gather(shards[25], "wa", axis=0, tiled=True),
        lax.all_gather(shards[26], "wa", axis=0, tiled=True),
        lax.all_gather(shards[27], "wa", axis=0, tiled=True),
    )
    back_weights = matrices(shaped(regathered))
    (
        back_receptance,
        back_key,
        back_value,
        back_output,
        back_down_decay,
        pullback_up_decay,
        back_down_rate,
        pullback_up_rate,
        pullback_down_value_residual,
        pullback_up_value_residual,
        back_down_gate,
        back_up_gate,
        back_hidden_in,
        back_hidden_out,
    ) = back_weights
    grad_out = unit_exit_slope.astype(jnp.float32)
    grad_hidden, grad_ffn_value = matrix_product_pullback(grad_out, hidden_low, back_hidden_out)
    grad_pre = grad_hidden * 2.0 * jax.nn.relu(pre_act)
    grad_channel, grad_ffn_key = matrix_product_pullback(grad_pre, channel_low, back_hidden_in)
    grad_normed_two, grad_before_two, grad_mix_channel = chan_back(grad_channel)
    grad_rows_two, grad_edge_two = prev_two_back(grad_before_two)
    edge_back_two = shifted_2(grad_edge_two, "sa", -1)
    grad_normed_two = (
        grad_normed_two
        + grad_rows_two
        + jnp.concatenate(
            [jnp.zeros((length - 1, model_width), jnp.float32), edge_back_two], axis=0
        )
    )
    grad_mid, grad_ln2_gain, grad_ln2_bias = ln_two_back(grad_normed_two)
    grad_mid = grad_mid + grad_out
    grad_mixed, grad_w_output = matrix_product_pullback(grad_mid, mixed_low, back_output)
    (
        grad_outputs,
        grad_recept_a,
        grad_key_mixed_a,
        grad_valued_a,
        grad_gate_rows,
        grad_lnx_gain,
        grad_lnx_bias,
        present_token_boost_slope,
    ) = finish_back(grad_mixed)
    grad_folded = fold(grad_outputs)
    span_grads = jnp.einsum("klhi,klhj->khij", grad_folded, carried, precision=HIGHEST)
    local_grad, unused_ends = lax.scan(back_step, zero_state, (span_maps, span_grads), reverse=True)
    later_map, later_grad = entering(
        (jnp.swapaxes(block_map, 1, 2), local_grad), "sa", chain_join, (identity, zero_state), True
    )
    unused_start, end_grads = lax.scan(back_step, later_grad, (span_maps, span_grads), reverse=True)
    state_grads = jax.vmap(span_back)(start_states, folded, keep_folded, grad_folded, end_grads)
    state_grads = tuple(
        (tensor_entry.reshape((length, head_count, HEAD_SIZE)) for tensor_entry in state_grads)
    )
    prep_grads = (
        state_grads[0] + grad_recept_a,
        state_grads[1],
        state_grads[2] + grad_key_mixed_a,
        state_grads[3] + grad_valued_a,
        state_grads[4],
        state_grads[5],
    )
    (
        grad_recept,
        grad_key_rows,
        grad_value_raw,
        decay_lowrank_output_gradient,
        value_residual_lowrank_gradient,
        rate_lowrank_output_gradient,
        grad_first,
        grad_decay_base,
        grad_rate_base,
        value_residual_logits_gradient,
        grad_key_norm,
        grad_key_rate,
    ) = prepare_back(prep_grads)
    grad_gate_low, grad_gate_up = matrix_product_pullback(grad_gate_rows, gate_low, back_up_gate)
    grad_gate_in, grad_gate_down = matrix_product_pullback(
        grad_gate_low * gate_sig * (1.0 - gate_sig), gate_in, back_down_gate
    )
    value_residual_hidden_gradient, value_residual_second_gradient = matrix_product_pullback(
        value_residual_lowrank_gradient, value_residual_hidden, pullback_up_value_residual
    )
    value_input_gradient_first, value_residual_first_gradient = matrix_product_pullback(
        value_residual_hidden_gradient, value_input_rows, pullback_down_value_residual
    )
    rate_hidden_gradient, rate_second_factor_gradient = matrix_product_pullback(
        rate_lowrank_output_gradient, rate_hidden_rows, pullback_up_rate
    )
    grad_rate_in, grad_rate_down = matrix_product_pullback(
        rate_hidden_gradient, rate_input_rows, back_down_rate
    )
    decay_lowrank_hidden_gradient, decay_second_factor_gradient = matrix_product_pullback(
        decay_lowrank_output_gradient, decay_lowrank_hidden, pullback_up_decay
    )
    grad_decay_in, grad_decay_down = matrix_product_pullback(
        decay_lowrank_hidden_gradient * (1.0 - decay_hidden * decay_hidden),
        decay_input_rows,
        back_down_decay,
    )
    grad_recept_in, grad_w_receptance = matrix_product_pullback(
        grad_recept, recept_in, back_receptance
    )
    grad_key_in, grad_w_key = matrix_product_pullback(grad_key_rows, key_in, back_key)
    grad_value_in_b, grad_w_value = matrix_product_pullback(
        grad_value_raw, value_input_rows, back_value
    )
    grad_normed_one, grad_before_one, grad_mix_time = mix_back(
        (
            grad_recept_in,
            grad_decay_in,
            grad_key_in,
            value_input_gradient_first + grad_value_in_b,
            grad_rate_in,
            grad_gate_in,
        )
    )
    grad_rows_one, grad_edge_one = prev_one_back(grad_before_one)
    edge_back_one = shifted_2(grad_edge_one, "sa", -1)
    grad_normed_one = (
        grad_normed_one
        + grad_rows_one
        + jnp.concatenate(
            [jnp.zeros((length - 1, model_width), jnp.float32), edge_back_one], axis=0
        )
    )
    grad_input, grad_ln1_gain, grad_ln1_bias = ln_one_back(grad_normed_one)
    grad_input = grad_input + grad_mid
    flat_grads = tuple(
        (
            tensor_entry.reshape(-1)
            for tensor_entry in (
                grad_ln1_gain,
                grad_ln1_bias,
                grad_mix_time,
                grad_w_receptance,
                grad_w_key,
                grad_w_value,
                grad_w_output,
                grad_decay_base,
                grad_decay_down,
                decay_second_factor_gradient,
                grad_rate_base,
                grad_rate_down,
                rate_second_factor_gradient,
                value_residual_logits_gradient,
                value_residual_first_gradient,
                value_residual_second_gradient,
                grad_gate_down,
                grad_gate_up,
                grad_key_norm,
                grad_key_rate,
                present_token_boost_slope,
                grad_lnx_gain,
                grad_lnx_bias,
                grad_ln2_gain,
                grad_ln2_bias,
                grad_mix_channel,
                grad_ffn_key,
                grad_ffn_value,
            )
        )
    )
    owned = lax.psum_scatter(flat_grads, "wa", scatter_dimension=0, tiled=True)
    summed = tuple(
        jax.tree.map(lambda part: part.astype(jnp.float32), lax.psum(shortened(owned), "sa"))
    )
    return (block_out.astype(jnp.bfloat16), grad_input, grad_first) + summed


def solution(mesh):
    return jax.shard_map(
        body,
        mesh=mesh,
        in_specs=(
            P(("wa", "sa"), None),
            P(("wa", "sa"), None),
            P(("wa", "sa")),
            P(("wa", "sa"), None),
            P("wa"),
            P("wa"),
            P("wa"),
            P("wa"),
            P("wa"),
            P("wa"),
            P("wa"),
            P("wa"),
            P("wa"),
            P("wa"),
            P("wa"),
            P("wa"),
            P("wa"),
            P("wa"),
            P("wa"),
            P("wa"),
            P("wa"),
            P("wa"),
            P("wa"),
            P("wa"),
            P("wa"),
            P("wa"),
            P("wa"),
            P("wa"),
            P("wa"),
            P("wa"),
            P("wa"),
            P("wa"),
        ),
        out_specs=(
            P(("wa", "sa"), None),
            P(("wa", "sa"), None),
            P(("wa", "sa"), None),
            P("wa"),
            P("wa"),
            P("wa"),
            P("wa"),
            P("wa"),
            P("wa"),
            P("wa"),
            P("wa"),
            P("wa"),
            P("wa"),
            P("wa"),
            P("wa"),
            P("wa"),
            P("wa"),
            P("wa"),
            P("wa"),
            P("wa"),
            P("wa"),
            P("wa"),
            P("wa"),
            P("wa"),
            P("wa"),
            P("wa"),
            P("wa"),
            P("wa"),
            P("wa"),
            P("wa"),
            P("wa"),
        ),
        check_vma=False,
    )
```

profile of v0, /device:TPU:0, one launch (start us, length us, event | category | flops | bytes accessed | tf_op | source)
XLA Modules:
  0.0 4898.8 jit_solution(1673867046783041848)
XLA Ops:
  15.2 21.6 all-gather.6
  36.8 16.3 all-gather.5
  55.4 18.3 all-gather.14
  74.3 30.5 all-gather.7
  105.6 16.2 all-gather.11
  122.4 31.0 all_gather.131
  153.6 31.0 all_gather.132
  184.6 18.1 all-gather.9
  203.3 16.5 all-gather.8
  221.0 31.1 all_gather.135
  252.2 31.0 all_gather.136
  283.3 18.0 all-gather.10
  302.0 16.7 all-gather.13
  319.3 17.9 all-gather.12
  338.5 31.3 all_gather.127
  370.5 31.2 all_gather.126
  401.8 16.5 all-gather.4
  418.3 32.1 all_gather.147
  451.3 31.8 all_gather.146
  483.6 18.2 all-gather.17
  502.4 16.1 all-gather.16
  519.1 18.2 all-gather.15
  595.2 776.2 %while.276 = (s32[]{:T(128)}, f32[4,16,64,64]{3,2,1,0:T(8,128)S(1)}, f32[4,16,64,64]{3,2,1,0:T(8,128)}, f32[32,4,16,64]{3,0,2,1:T(8,128)}, f32[32,4,16,64]{3,2,1...) while((s32[]{:T(128)}, f32[4,16,64,64]{3,2,1,0:T(8,128)S(1)}, ...), condition=%wide.region_8.9_spmd.clone, body=%wide.region_3.8_spmd.clone.sunk | while | flops 5243009 | bytes 14483983 | solution.py:268
  627.4 9.6 multiply_add_fusion.20
  1372.2 35.7 while.277
  1408.8 11.8 all-gather
  1421.4 12.0 all-gather.1
  1433.4 10.8 while.278
  1507.7 337.4 %while.272 = (s32[]{:T(128)}, f32[4,16,64,64]{3,2,1,0:T(8,128)S(1)}, f32[8,4,16,64,64]{4,3,2,1,0:T(8,128)}, f32[8,4,4,16,64]{4,3,1,2,0:T(8,128)}, f32[8,4,4,16,6...) while((s32[]{:T(128)}, f32[4,16,64,64]{3,2,1,0:T(8,128)S(1)}, ...), condition=%wide.region_32.33_spmd, body=%wide.region_28.32_spmd.sunk | while | flops 2101315 | bytes 8241798 | solution.py:225
  1514.1 35.7 while.281
  1556.3 35.7 while.281
  1598.5 35.7 while.281
  1640.6 35.7 while.281
  1682.8 35.7 while.281
  1725.0 35.7 while.281
  1767.2 35.7 while.281
  1809.4 35.7 while.281
  1846.4 11.0 all-gather.2
  1863.9 13.3 reshape.674
  1890.1 13.3 reshape.675
  1958.0 14.2 while.279
  1973.5 11.6 all-gather.3
  1985.1 11.0 while.280
  1997.7 14.7 while.270
  2022.5 627.4 %while.275 = (s32[]{:T(128)}, f32[4,16,64,64]{3,2,1,0:T(8,128)}, f32[8,4,4,16,64]{4,3,1,2,0:T(8,128)}, f32[8,4,4,16,64]{4,3,1,2,0:T(8,128)}, f32[8,4,4,16,64]{4,...) while((s32[]{:T(128)}, f32[4,16,64,64]{3,2,1,0:T(8,128)}, ...), condition=%wide.region_46.47_spmd, body=%wide.region_33.46_spmd.sunk | while | flops 8617992 | bytes 19252708 | solution.py:225
  2032.3 20.3 while.282
  2052.7 46.0 while.283
  2110.7 20.3 while.282
  2131.1 46.0 while.283
  2189.1 20.3 while.282
  2209.5 46.0 while.283
  2267.5 20.3 while.282
  2287.9 46.0 while.283
  2345.9 20.3 while.282
  2366.4 46.0 while.283
  2424.4 20.3 while.282
  2444.8 46.0 while.283
  2502.8 20.3 while.282
  2523.2 46.0 while.283
  2581.2 20.3 while.282
  2601.6 46.0 while.283
  2739.9 2018.4 %all-reduce.48 = (bf16[1024]{0:T(1024)(128)(2,1)S(1)}, bf16[1024]{0:T(1024)(128)(2,1)S(1)}, bf16[6144]{0:T(1024)(128)(2,1)S(1)}, bf16[1048576]{0:T(1024)(128)(2,...) all-reduce(f32[1024]{0:T(1024)S(1)} %get-tuple-element.2018, ...), channel_id=6, replica_groups=mesh['wa'=8,'sa'=4] {'wa'}, use_global_device_ids=true, to_apply=%region_52.53.clone | all-reduce | flops 13257728 | bytes 79546368
  4796.0 10.5 all-reduce.45.cloned.1.call-done
  4833.6 48.6 all-reduce.47.cloned.1.call-done
  (2971 shorter events, 2194.8 us)
Async XLA Ops:
  7.2 29.6 copy-start.210
  7.2 45.8 copy-start.13
  7.3 552.0 %all-gather.25.cloned.1.call-start = ((), (), s32[]{:S(2)}) async-start(), calls=%async_computation | async-start | bytes 2359296 | tf_op jit(solution)/shard_map/all_gather | solution.py:385
  8.0 556.3 %all-gather.29.cloned.1.call-start = ((), (), s32[]{:S(2)}) async-start(), calls=%async_computation.2 | async-start | bytes 2359296 | tf_op jit(solution)/shard_map/all_gather | solution.py:384
  8.7 46.7 copy-start.211
  8.7 65.6 %copy-start.203 = (bf16[768]{0:T(1024)(128)(2,1)S(1)}, bf16[768]{0:T(1024)(128)(2,1)}, u32[]{:S(2)}) copy-start(bf16[768]{0:T(1024)(128)(2,1)} %param.60) | copy-start | bytes 4612
  8.8 96.8 %copy-start.212 = (bf16[128]{0:T(256)(128)(2,1)S(1)}, bf16[128]{0:T(256)(128)(2,1)}, u32[]{:S(2)}) copy-start(bf16[128]{0:T(256)(128)(2,1)} %param.77) | copy-start | bytes 772
  8.8 113.7 %copy-start.187 = (bf16[8192]{0:T(1024)(128)(2,1)S(1)}, bf16[8192]{0:T(1024)(128)(2,1)}, u32[]{:S(2)}) copy-start(bf16[8192]{0:T(1024)(128)(2,1)} %param.69) | copy-start | bytes 49156
  8.8 565.3 %all-gather.27.cloned.1.call-start = ((), (), s32[]{:S(2)}) async-start(), calls=%async_computation.1 | async-start | bytes 2359296 | tf_op jit(solution)/shard_map/all_gather | solution.py:386
  9.5 1479.9 %all-gather.31.cloned.1.call-start = ((), (), s32[]{:S(2)}) async-start(), calls=%async_computation.3 | async-start | bytes 2359296 | tf_op jit(solution)/shard_map/all_gather | solution.py:387
  10.1 143.5 %copy-start.188 = (bf16[8192]{0:T(1024)(128)(2,1)S(1)}, bf16[8192]{0:T(1024)(128)(2,1)}, u32[]{:S(2)}) copy-start(bf16[8192]{0:T(1024)(128)(2,1)} %param.70) | copy-start | bytes 49156
  10.1 174.5 %copy-start.213 = (bf16[128]{0:T(256)(128)(2,1)S(1)}, bf16[128]{0:T(256)(128)(2,1)}, u32[]{:S(2)}) copy-start(bf16[128]{0:T(256)(128)(2,1)} %param.68) | copy-start | bytes 772
  10.1 193.2 %copy-start.214 = (bf16[128]{0:T(256)(128)(2,1)S(1)}, bf16[128]{0:T(256)(128)(2,1)}, u32[]{:S(2)}) copy-start(bf16[128]{0:T(256)(128)(2,1)} %param.76) | copy-start | bytes 772
  10.1 1853.7 %all-gather.33.cloned.1.call-start = ((), (), s32[]{:S(2)}) async-start(), calls=%async_computation.4 | async-start | bytes 9437184 | tf_op jit(solution)/shard_map/all_gather | solution.py:407
  10.7 210.3 %copy-start.198 = (bf16[4096]{0:T(1024)(128)(2,1)S(1)}, bf16[4096]{0:T(1024)(128)(2,1)}, u32[]{:S(2)}) copy-start(bf16[4096]{0:T(1024)(128)(2,1)} %param.72) | copy-start | bytes 24580
  10.7 241.5 %copy-start.199 = (bf16[4096]{0:T(1024)(128)(2,1)S(1)}, bf16[4096]{0:T(1024)(128)(2,1)}, u32[]{:S(2)}) copy-start(bf16[4096]{0:T(1024)(128)(2,1)} %param.73) | copy-start | bytes 24580
  10.7 1879.4 %all-gather.35.cloned.1.call-start = ((), (), s32[]{:S(2)}) async-start(), calls=%async_computation.5 | async-start | bytes 9437184 | tf_op jit(solution)/shard_map/all_gather | solution.py:408
  12.0 529.7 %collective-permute-start = (f32[1]{0:T(128)}, f32[1]{0:T(128)}, u32[]{:S(2)}, u32[]{:S(2)}) collective-permute-start(f32[1]{0:T(128)} %convert_element_type.360), channel_id=1, source_target_pairs={{0,1},{1,2},{2,3},{4,5},{5,6},{6,7},{8,9},{9,10},{10,11},{12,13},{... | collective-permute-start | bytes 20 | tf_op jit(solution)/shard_map/ppermute | solution.py:26
  53.1 492.5 %copy-start.135 = (f32[8,1,128]{2,1,0:T(1,128)}, f32[8,1,128]{2,1,0:T(1,128)S(1)}, u32[]{:S(2)}) copy-start(f32[8,1,128]{2,1,0:T(1,128)S(1)} %convert_element_type.467) | copy-start | bytes 12292
  53.1 230.2 %copy-start.215 = (bf16[128]{0:T(256)(128)(2,1)S(1)}, bf16[128]{0:T(256)(128)(2,1)}, u32[]{:S(2)}) copy-start(bf16[128]{0:T(256)(128)(2,1)} %param.71) | copy-start | bytes 772
  53.1 248.8 %copy-start.216 = (bf16[128]{0:T(256)(128)(2,1)S(1)}, bf16[128]{0:T(256)(128)(2,1)}, u32[]{:S(2)}) copy-start(bf16[128]{0:T(256)(128)(2,1)} %param.80) | copy-start | bytes 772
  53.1 266.1 %copy-start.217 = (bf16[128]{0:T(256)(128)(2,1)S(1)}, bf16[128]{0:T(256)(128)(2,1)}, u32[]{:S(2)}) copy-start(bf16[128]{0:T(256)(128)(2,1)} %param.79) | copy-start | bytes 772
  53.3 285.2 %copy-start.189 = (bf16[8192]{0:T(1024)(128)(2,1)S(1)}, bf16[8192]{0:T(1024)(128)(2,1)}, u32[]{:S(2)}) copy-start(bf16[8192]{0:T(1024)(128)(2,1)} %param.67) | copy-start | bytes 49156
  53.3 492.3 %copy-start.180 = (f32[128]{0:T(128)}, f32[128]{0:T(128)S(1)}, u32[]{:S(2)}) copy-start(f32[128]{0:T(128)S(1)} %broadcast_multiply_fusion.4) | copy-start | bytes 1540
  53.5 20.8 copy-start.207
  53.5 492.1 %copy-start.193 = (f32[128]{0:T(128)}, f32[128]{0:T(128)S(1)}, u32[]{:S(2)}) copy-start(f32[128]{0:T(128)S(1)} %fusion.149) | copy-start | bytes 1540
  53.5 316.9 %copy-start.190 = (bf16[8192]{0:T(1024)(128)(2,1)S(1)}, bf16[8192]{0:T(1024)(128)(2,1)}, u32[]{:S(2)}) copy-start(bf16[8192]{0:T(1024)(128)(2,1)} %param.66) | copy-start | bytes 49156
  53.8 348.0 %copy-start.218 = (bf16[128]{0:T(256)(128)(2,1)S(1)}, bf16[128]{0:T(256)(128)(2,1)}, u32[]{:S(2)}) copy-start(bf16[128]{0:T(256)(128)(2,1)} %param.65) | copy-start | bytes 772
  53.8 364.5 %copy-start.168 = (bf16[20480]{0:T(1024)(128)(2,1)S(1)}, bf16[20480]{0:T(1024)(128)(2,1)}, u32[]{:S(2)}) copy-start(bf16[20480]{0:T(1024)(128)(2,1)} %param.75) | copy-start | bytes 122884
  53.8 490.1 %collective-permute-start.1 = (f32[1,1024]{1,0:T(1,128)S(1)}, f32[1,1024]{1,0:T(1,128)S(1)}, u32[]{:S(2)}, u32[]{:S(2)}) collective-permute-start(f32[1,1024]{1,0:T(1,128)S(1)} %slice.62), channel_id=1, source_target_pairs={{0,1},{1,2},{2,3},{4,5},{5,6},{6,7},{8,9},{9,10},{10,11},{12,13},{... | collective-permute-start | bytes 12296 | tf_op jit(solution)/shard_map/ppermute | solution.py:26
  55.1 396.2 %copy-start.169 = (bf16[20480]{0:T(1024)(128)(2,1)S(1)}, bf16[20480]{0:T(1024)(128)(2,1)}, u32[]{:S(2)}) copy-start(bf16[20480]{0:T(1024)(128)(2,1)} %param.74) | copy-start | bytes 122884
  55.2 4751.4 %all-reduce.45.cloned.1.call-start = ((), (), s32[]{:S(2)}) async-start(), calls=%async_computation.6 | async-start | bytes 345088 | tf_op jit(solution)/shard_map/psum | solution.py:755
  55.3 427.8 %copy-start.125 = (f32[64,64]{0,1:T(8,128)}, f32[64,64]{0,1:T(8,128)S(1)}, u32[]{:S(2)}) copy-start(f32[64,64]{0,1:T(8,128)S(1)} %fusion.143) | copy-start | bytes 49156
  104.9 439.6 %copy-start.158 = (f32[1024]{0:T(1024)}, f32[1024]{0:T(1024)S(1)}, u32[]{:S(2)}) copy-start(f32[1024]{0:T(1024)S(1)} %get-tuple-element.2393) | copy-start | bytes 12292
  104.9 440.7 %copy-start.156 = (f32[1024]{0:T(1024)}, f32[1024]{0:T(1024)S(1)}, u32[]{:S(2)}) copy-start(f32[1024]{0:T(1024)S(1)} %get-tuple-element.2392) | copy-start | bytes 12292
  104.9 440.7 %copy-start.160 = (f32[1024]{0:T(1024)}, f32[1024]{0:T(1024)S(1)}, u32[]{:S(2)}) copy-start(f32[1024]{0:T(1024)S(1)} %get-tuple-element.2394) | copy-start | bytes 12292
  104.9 440.7 %copy-start.162 = (f32[1024]{0:T(1024)}, f32[1024]{0:T(1024)S(1)}, u32[]{:S(2)}) copy-start(f32[1024]{0:T(1024)S(1)} %get-tuple-element.2395) | copy-start | bytes 12292
  104.9 440.7 %copy-start.164 = (f32[1024]{0:T(1024)}, f32[1024]{0:T(1024)S(1)}, u32[]{:S(2)}) copy-start(f32[1024]{0:T(1024)S(1)} %get-tuple-element.2396) | copy-start | bytes 12292
  104.9 440.7 %copy-start.166 = (f32[1024]{0:T(1024)}, f32[1024]{0:T(1024)S(1)}, u32[]{:S(2)}) copy-start(f32[1024]{0:T(1024)S(1)} %get-tuple-element.2397) | copy-start | bytes 12292
  153.6 399.8 %copy-start.85 = (bf16[1024,64]{1,0:T(8,128)(2,1)}, bf16[1024,64]{1,0:T(8,128)(2,1)S(1)}, u32[]{:S(2)}) copy-start(bf16[1024,64]{1,0:T(8,128)(2,1)S(1)} %reshape.660) | copy-start | bytes 393220
  184.5 299.1 %copy-start.219 = (bf16[128]{0:T(256)(128)(2,1)S(1)}, bf16[128]{0:T(256)(128)(2,1)}, u32[]{:S(2)}) copy-start(bf16[128]{0:T(256)(128)(2,1)} %param.83) | copy-start | bytes 772
  184.5 317.8 %copy-start.220 = (bf16[128]{0:T(256)(128)(2,1)S(1)}, bf16[128]{0:T(256)(128)(2,1)}, u32[]{:S(2)}) copy-start(bf16[128]{0:T(256)(128)(2,1)} %param.82) | copy-start | bytes 772
  184.5 334.6 %copy-start.221 = (bf16[128]{0:T(256)(128)(2,1)S(1)}, bf16[128]{0:T(256)(128)(2,1)}, u32[]{:S(2)}) copy-start(bf16[128]{0:T(256)(128)(2,1)} %param.81) | copy-start | bytes 772
  184.5 353.3 %copy-start.224 = (u32[32]{0:T(128)S(1)}, u32[32]{0:T(128)}, u32[]{:S(2)}) copy-start(u32[32]{0:T(128)} %constant.426) | copy-start | bytes 388
  184.6 369.0 %copy-start.123 = (bf16[64,1024]{1,0:T(8,128)(2,1)}, bf16[64,1024]{1,0:T(8,128)(2,1)S(1)}, u32[]{:S(2)}) copy-start(bf16[64,1024]{1,0:T(8,128)(2,1)S(1)} %reshape.661) | copy-start | bytes 393220
  252.2 305.3 %copy-start.83 = (bf16[1024,32]{1,0:T(8,128)(2,1)}, bf16[1024,32]{1,0:T(8,128)(2,1)S(1)}, u32[]{:S(2)}) copy-start(bf16[1024,32]{1,0:T(8,128)(2,1)S(1)} %reshape.664) | copy-start | bytes 196612
  283.3 274.8 %copy-start.131 = (bf16[32,1024]{1,0:T(8,128)(2,1)}, bf16[32,1024]{1,0:T(8,128)(2,1)S(1)}, u32[]{:S(2)}) copy-start(bf16[32,1024]{1,0:T(8,128)(2,1)S(1)} %reshape.665) | copy-start | bytes 196612
  401.8 145.2 %copy-start.87 = (bf16[1024,64]{1,0:T(8,128)(2,1)}, bf16[1024,64]{1,0:T(8,128)(2,1)S(1)}, u32[]{:S(2)}) copy-start(bf16[1024,64]{1,0:T(8,128)(2,1)S(1)} %reshape.654) | copy-start | bytes 393220
  483.6 74.2 %copy-start.44 = (bf16[1024,160]{1,0:T(8,128)(2,1)}, bf16[1024,160]{1,0:T(8,128)(2,1)S(1)}, u32[]{:S(2)}) copy-start(bf16[1024,160]{1,0:T(8,128)(2,1)S(1)} %reshape.671) | copy-start | bytes 983044
  558.1 928.1 %copy-start.110 = (f32[128,160]{0,1:T(8,128)}, f32[128,160]{0,1:T(8,128)S(1)}, u32[]{:S(2)}) copy-start(f32[128,160]{0,1:T(8,128)S(1)} %fusion.92) | copy-start | bytes 245764
  1407.9 25.5 copy-start
  1408.8 24.7 copy-start.26
  1457.0 493.2 %copy-start.7 = (f32[4,32,16,64]{3,1,2,0:T(8,128)}, f32[4,32,16,64]{3,1,2,0:T(8,128)S(1)}, u32[]{:S(2)}) copy-start(f32[4,32,16,64]{3,1,2,0:T(8,128)S(1)} %get-tuple-element.2406) | copy-start | bytes 1572868
  1459.3 16.7 copy-start.127
  1498.3 363.8 %collective-permute-start.2 = (f32[1,1024]{1,0:T(1,128)}, f32[1,1024]{1,0:T(1,128)}, u32[]{:S(2)}, u32[]{:S(2)}) collective-permute-start(f32[1,1024]{1,0:T(1,128)} %slice.70), channel_id=1, source_target_pairs={{0,1},{1,2},{2,3},{4,5},{5,6},{6,7},{8,9},{9,10},{10,11},{12,13},{... | collective-permute-start | bytes 12296 | tf_op jit(solution)/shard_map/ppermute | solution.py:26
  1846.3 15.8 copy-start.10
  1846.3 15.8 copy-start.34
  1846.4 15.8 copy-start.146
  1846.4 15.8 copy-start.153
  1846.4 15.8 copy-start.171
  1882.0 21.5 copy-start.3
  1916.8 23.7 collective-permute-start.3
  2706.3 30.1 collective-permute-start.4
  4775.8 106.4 %all-reduce.47.cloned.1.call-start = ((), (), s32[]{:S(2)}) async-start(), calls=%async_computation.7 | async-start | bytes 6291456 | tf_op jit(solution)/shard_map/psum | solution.py:755
  (433 other events, 1790.5 us)
Sparse Core Ops, SparseCore 0:
  10.2 52.0 all-gather.24
  64.4 47.9 all-gather.28
  114.6 49.1 all-gather.26
  165.8 48.2 all-gather.30
  216.1 126.2 all-gather.32
  344.3 130.7 all-gather.34
  4775.9 30.5 all-reduce.44
  4811.2 70.9 all-reduce.46
where the time goes:
time: 4940 us; the launch traced here: 4900 us
  blocking collectives  2570 us (52%)
  other arithmetic  1100 us (22%)
  local copies, waits for them, and re-layouts  970 us (20%)
  matrix products  147 us (3%)
  waiting for transfers between devices  62.3 us (1%)
    unnamed x1, blocking collectives  2020 us
    mul x32, other arithmetic, pair_step(): jnp.sum(current * standardized_lines[:, None, :], axis=2, keepdims=True)  307 us
    mul x32, other arithmetic, state_step(): jnp.sum(current * standardized_lines[:, None, :], axis=2, keepdims=True)  232 us
    reduce_sum x32, other arithmetic, state_step(): current * standardized_lines[:, None, :]  209 us
    while x656, local copies, waits for them, and re-layouts  158 us
    reduce_sum x64, other arithmetic, state_step(): jnp.sum(current * standardized_lines[:, None, :], axis=2, keepdims=True)  104 us
  transfers between devices with their start and end apart: 13, of which 2 were waited for; matrix products, arithmetic and copies ran while one was open for 28% of the time, Pallas kernels for 0%

commit v1 on v0

--- a/solution.py
+++ b/solution.py
@@ -1,5 +1,3 @@
-import math
-
 import jax
 import jax.numpy as jnp
 from jax import lax
@@ -15,6 +13,7 @@
 
 
 HIGHEST = lax.Precision.HIGHEST
+MATRIX_PRECISION = lax.Precision.HIGH
 DECAY_FACTOR = 0.606531
 CLUSTER_EPSILON = 0.00064
 NORM_EPS = 1e-05
@@ -26,36 +25,70 @@
     return lax.ppermute(block, axis, route)
 
 
-def entering(value, axis, combine, identity, reverse):
+BIG = (3, 4, 5, 6, 26, 27)
+
+
+def chain_states(block_map, block_shift, axis):
     devices, mine = (lax.axis_size(axis), lax.axis_index(axis))
-    everything = jax.tree.map(
-        lambda part, kind: lax.all_gather(part.astype(kind), axis),
-        value,
-        (jnp.bfloat16, jnp.bfloat16),
-    )
-    start = jax.tree.map(
-        lambda part, zero: jnp.broadcast_to(jnp.asarray(zero, part.dtype), part.shape),
-        value,
-        identity,
-    )
-
-    def hop(k, before):
-        at = devices - 1 - k if reverse else k
-        reached = at > mine if reverse else at < mine
-        new = combine(
-            before, jax.tree.map(lambda part, own: part[at].astype(own.dtype), everything, value)
-        )
-        return jax.tree.map(lambda a, b: jnp.where(reached, a, b), new, before)
-
-    return lax.fori_loop(0, devices, hop, start)
-
-
-def shortened(value):
-
-    def short(part):
-        return part.astype(jnp.bfloat16) if part.dtype == jnp.float32 else part
-
-    return jax.tree.map(short, value)
+    pair = jnp.stack([block_map, block_shift]).astype(jnp.bfloat16)
+    everything = lax.all_gather(pair, axis).astype(jnp.float32)
+    maps = everything[:, 0]
+    state = jnp.zeros_like(block_shift)
+    for k in range(devices - 1):
+        new = everything[k, 1]
+        if k:
+            new = new + jnp.einsum("hij,hjk->hik", state, maps[k], precision=HIGHEST)
+        state = jnp.where(k < mine, new, state)
+    return (maps, state)
+
+
+def chain_grads(maps, local_grad, axis):
+    devices, mine = (lax.axis_size(axis), lax.axis_index(axis))
+    everything = lax.all_gather(local_grad.astype(jnp.bfloat16), axis).astype(jnp.float32)
+    grad = jnp.zeros_like(local_grad)
+    for k in range(devices - 1, 0, -1):
+        new = everything[k]
+        if k < devices - 1:
+            new = new + jnp.einsum("hij,hlj->hil", grad, maps[k], precision=HIGHEST)
+        grad = jnp.where(k > mine, new, grad)
+    return grad
+
+
+def gather_weights(shards):
+    shapes = layout()
+    small = [i for i in range(len(shards)) if i not in BIG]
+    packed = lax.all_gather(jnp.concatenate([shards[i] for i in small]), "wa")
+    whole = [None] * len(shards)
+    at = 0
+    for i in small:
+        n = shards[i].shape[0]
+        whole[i] = packed[:, at : at + n].reshape(shapes[i])
+        at += n
+    for i in BIG:
+        whole[i] = lax.all_gather(shards[i].reshape(-1, shapes[i][1]), "wa", axis=0, tiled=True)
+    return tuple(whole)
+
+
+def reduce_big(grad):
+    part = lax.psum_scatter(grad.astype(jnp.bfloat16), "wa", scatter_dimension=0, tiled=True)
+    return lax.psum(part, "sa").reshape(-1).astype(jnp.float32)
+
+
+def reduce_small(grads):
+    owners = lax.axis_size("wa")
+    packed = jnp.concatenate(
+        [grad.astype(jnp.bfloat16).reshape(owners, -1) for grad in grads], axis=1
+    )
+    packed = jnp.pad(packed, ((0, 0), (0, -packed.shape[1] % 2048)))
+    part = lax.psum_scatter(packed.reshape(-1, 128), "wa", scatter_dimension=0, tiled=True)
+    total = lax.psum(part, "sa").reshape(-1).astype(jnp.float32)
+    out = []
+    at = 0
+    for grad in grads:
+        n = grad.size // owners
+        out.append(total[at : at + n])
+        at += n
+    return out
 
 
 def layout():
@@ -88,12 +121,6 @@
         (NETWORK_WIDTH,),
         (NETWORK_WIDTH, FEEDFORWARD_UNITS),
         (FEEDFORWARD_UNITS, NETWORK_WIDTH),
-    )
-
-
-def shaped(flat_parts):
-    return tuple(
-        (tensor_entry.reshape(target) for tensor_entry, target in zip(flat_parts, layout()))
     )
 
 
@@ -136,9 +163,7 @@
     erasure_lookup_stretch,
     stored_lookup_speed,
 ):
-    decay_factors = jnp.exp(
-        -DECAY_FACTOR * jax.nn.sigmoid(fading_feature_odds + decay_lowrank_output)
-    )
+    log_decay = -DECAY_FACTOR * jax.nn.sigmoid(fading_feature_odds + decay_lowrank_output)
     content_outcome_lines = unmixed_value_rows + (
         initial_layer_value - unmixed_value_rows
     ) * jax.nn.sigmoid(content_skip_odds + value_residual_lowrank)
@@ -154,7 +179,7 @@
     removal = standardized_lines * rate_sigmoid_gate.reshape(head_shape)
     return (
         acceptor_lines.reshape(head_shape),
-        decay_factors.reshape(head_shape),
+        log_decay.reshape(head_shape),
         lagged_lookup_entry.reshape(head_shape),
         content_outcome_lines.reshape(head_shape),
         standardized_lines,
@@ -188,114 +213,88 @@
     ) * valve_exit_lines
 
 
-def state_step(current, inputs):
-    (
-        acceptor_lines,
-        decay_factors,
-        keyed,
-        content_outcome_lines,
-        standardized_lines,
-        removal,
-        keeping,
-    ) = inputs
-    current = current * keeping
-    current = (
-        current * decay_factors[:, None, :]
-        - jnp.sum(current * standardized_lines[:, None, :], axis=2, keepdims=True)
-        * removal[:, None, :]
-        + content_outcome_lines[:, :, None] * keyed[:, None, :]
-    )
-    return (current, jnp.sum(current * acceptor_lines[:, None, :], axis=2))
-
-
-def sweep_block(current, block_inputs):
-    return lax.scan(state_step, current, block_inputs)
-
-
-def recurrence(initial, inputs, keeping):
-    length = keeping.shape[0]
-    block_size = math.gcd(length, 4)
-    blocks = length // block_size
-    folded = tuple(
-        (
-            tensor_entry.reshape((blocks, block_size) + tensor_entry.shape[1:])
-            for tensor_entry in inputs + (keeping,)
-        )
-    )
-    last_state, unit_outcomes = lax.scan(jax.checkpoint(sweep_block), initial, folded)
-    return (unit_outcomes.reshape((length,) + unit_outcomes.shape[2:]), last_state)
-
-
-def pair_step(carry, inputs):
-    transit, current = carry
-    (
-        acceptor_lines,
-        decay_factors,
-        keyed,
-        content_outcome_lines,
-        standardized_lines,
-        removal,
-        keeping,
-    ) = inputs
-    transit = transit * keeping
-    current = current * keeping
-    transit = (
-        transit * decay_factors[:, None, :]
-        - jnp.sum(transit * standardized_lines[:, None, :], axis=2, keepdims=True)
-        * removal[:, None, :]
-    )
-    current = (
-        current * decay_factors[:, None, :]
-        - jnp.sum(current * standardized_lines[:, None, :], axis=2, keepdims=True)
-        * removal[:, None, :]
-        + content_outcome_lines[:, :, None] * keyed[:, None, :]
-    )
-    return (
-        (transit, current),
-        (
-            jnp.sum(current * acceptor_lines[:, None, :], axis=2),
-            jnp.sum(transit * acceptor_lines[:, None, :], axis=2),
-        ),
-    )
-
-
-def span_sweep(inputs, keep_span):
-    head_count = inputs[0].shape[1]
-    identity = jnp.broadcast_to(
-        jnp.eye(HEAD_SIZE, dtype=jnp.float32), (head_count, HEAD_SIZE, HEAD_SIZE)
-    )
-    zero_state = jnp.zeros((head_count, HEAD_SIZE, HEAD_SIZE), jnp.float32)
-    (span_map, span_shift), (local_out, carried) = lax.scan(
-        pair_step, (identity, zero_state), inputs + (keep_span,)
-    )
+def batched(spec, left, right):
+    return jnp.einsum(spec, left, right, precision=MATRIX_PRECISION)
+
+
+def unit_lower_inverse(low):
+    size = low.shape[-1]
+    rows = lax.broadcasted_iota(jnp.int32, (size, size), 0)
+    cols = lax.broadcasted_iota(jnp.int32, (size, size), 1)
+
+    def corner(span):
+        return (rows // (2 * span) == cols // (2 * span)) & (rows // span > cols // span)
+
+    found = jnp.where(rows == cols, 1.0, 0.0) - jnp.where(corner(1), low, 0.0)
+    span = 2
+    while span < size:
+        below = jnp.where(corner(span), low, 0.0)
+        found = found - batched("htm,hms->hts", batched("htm,hms->hts", found, below), found)
+        span *= 2
+    return found
+
+
+@jax.custom_vjp
+def triangle_solve(low, right):
+    return batched("hts,hsj->htj", unit_lower_inverse(low), right)
+
+
+def triangle_forward(low, right):
+    inverse = unit_lower_inverse(low)
+    solved = batched("hts,hsj->htj", inverse, right)
+    return (solved, (inverse, solved))
+
+
+def triangle_backward(kept, grad):
+    inverse, solved = kept
+    grad_right = batched("hts,htj->hsj", inverse, grad)
+    return (-batched("htj,hsj->hts", grad_right, solved), grad_right)
+
+
+triangle_solve.defvjp(triangle_forward, triangle_backward)
+
+
+def block_sweep(recept, log_decay, keyed, valued, kappa, removal, keeping):
+    length, width = (recept.shape[0], recept.shape[2])
+    recept, log_decay, keyed, valued, kappa, removal = (
+        jnp.swapaxes(part, 0, 1)
+        for part in (recept, log_decay, keyed, valued, kappa, removal)
+    )
+    rows = lax.broadcasted_iota(jnp.int32, (length, length), 0)
+    cols = lax.broadcasted_iota(jnp.int32, (length, length), 1)
+    upto = jnp.where(cols <= rows, 1.0, 0.0)
+    resets = jnp.sum(upto * (1.0 - keeping)[None, :], axis=1)
+    same = resets[:, None] == resets[None, :]
+    reached = jnp.where(resets == 0, 1.0, 0.0)[:, None]
+    lasting = jnp.where(resets == resets[-1], 1.0, 0.0)[:, None]
+    total = jnp.einsum("ts,hsj->htj", upto, log_decay, precision=HIGHEST)
+    middle = lax.stop_gradient(total[:, length // 2 - 1 : length // 2])
+    rising = jnp.exp(total - middle)
+    queries = jnp.concatenate([kappa * jnp.exp(total - log_decay - middle), recept * rising], 1)
+    falling = jnp.exp(middle - total)
+    keys = jnp.concatenate([keyed * falling, removal * falling], 1)
+    scores = batched("htj,hsj->hts", queries, keys)
+    before = same & (cols < rows)
+    until = same & (cols <= rows)
+    write_to_kappa = jnp.where(before, scores[:, :length, :length], 0.0)
+    erase_to_kappa = jnp.where(before, scores[:, :length, length:], 0.0)
+    write_to_out = jnp.where(until, scores[:, length:, :length], 0.0)
+    erase_to_out = jnp.where(until, scores[:, length:, length:], 0.0)
+    entering_kappa = reached * kappa * jnp.exp(total - log_decay)
+    entering_out = reached * recept * jnp.exp(total)
+    solved = triangle_solve(
+        erase_to_kappa,
+        jnp.concatenate([entering_kappa, batched("hts,hsi->hti", write_to_kappa, valued)], 2),
+    )
+    erased = batched("hts,hsj->htj", erase_to_out, solved)
+    carried = entering_out - erased[:, :, :width]
+    local_out = batched("hts,hsi->hti", write_to_out, valued) - erased[:, :, width:]
+    ending = lasting * jnp.exp(total[:, -1:] - total)
+    erasing = batched("hsi,hsj->hij", solved, removal * ending)
+    end_decay = reached[-1, 0] * jnp.exp(total[:, -1])
+    span_map = jnp.eye(width, dtype=jnp.float32) * end_decay[:, None, :] - erasing[:, :width]
+    span_shift = batched("hsi,hsj->hij", valued, keyed * ending) - erasing[:, width:]
     return (span_map, span_shift, local_out, carried)
-
-
-def span_back(initial, inputs, keep_span, grad_span, end_grad):
-
-    def run_span(start, *members):
-        return recurrence(start, members, keep_span)
-
-    unused, pullback = jax.vjp(run_span, initial, *inputs)
-    return pullback((grad_span, end_grad))[1:]
-
-
-def chain_join(earlier, later):
-    first_map, first_shift = earlier
-    second_map, second_shift = later
-    joined = jnp.einsum("hij,hjk->hik", first_map, second_map, precision=HIGHEST)
-    shifted = jnp.einsum("hij,hjk->hik", first_shift, second_map, precision=HIGHEST) + second_shift
-    return (joined, shifted)
-
-
-def prefix_step(carry, tensor_entry):
-    return (chain_join(carry, tensor_entry), carry)
-
-
-def back_step(end_grad, tensor_entry):
-    span_map, span_grad = tensor_entry
-    start_grad = span_grad + jnp.einsum("hij,hlj->hil", end_grad, span_map, precision=HIGHEST)
-    return (start_grad, end_grad)
 
 
 def matrix_multiply(left, right):
@@ -377,37 +376,7 @@
         perceptron_lookup_array,
         perceptron_content_array,
     )
-    gathered = (
-        lax.all_gather(shards[0], "wa", axis=0, tiled=True),
-        lax.all_gather(shards[1], "wa", axis=0, tiled=True),
-        lax.all_gather(shards[2], "wa", axis=0, tiled=True),
-        lax.all_gather(shards[3], "wa", axis=0, tiled=True),
-        lax.all_gather(shards[4], "wa", axis=0, tiled=True),
-        lax.all_gather(shards[5], "wa", axis=0, tiled=True),
-        lax.all_gather(shards[6], "wa", axis=0, tiled=True),
-        lax.all_gather(shards[7], "wa", axis=0, tiled=True),
-        lax.all_gather(shards[8], "wa", axis=0, tiled=True),
-        lax.all_gather(shards[9], "wa", axis=0, tiled=True),
-        lax.all_gather(shards[10], "wa", axis=0, tiled=True),
-        lax.all_gather(shards[11], "wa", axis=0, tiled=True),
-        lax.all_gather(shards[12], "wa", axis=0, tiled=True),
-        lax.all_gather(shards[13], "wa", axis=0, tiled=True),
-        lax.all_gather(shards[14], "wa", axis=0, tiled=True),
-        lax.all_gather(shards[15], "wa", axis=0, tiled=True),
-        lax.all_gather(shards[16], "wa", axis=0, tiled=True),
-        lax.all_gather(shards[17], "wa", axis=0, tiled=True),
-        lax.all_gather(shards[18], "wa", axis=0, tiled=True),
-        lax.all_gather(shards[19], "wa", axis=0, tiled=True),
-        lax.all_gather(shards[20], "wa", axis=0, tiled=True),
-        lax.all_gather(shards[21], "wa", axis=0, tiled=True),
-        lax.all_gather(shards[22], "wa", axis=0, tiled=True),
-        lax.all_gather(shards[23], "wa", axis=0, tiled=True),
-        lax.all_gather(shards[24], "wa", axis=0, tiled=True),
-        lax.all_gather(shards[25], "wa", axis=0, tiled=True),
-        lax.all_gather(shards[26], "wa", axis=0, tiled=True),
-        lax.all_gather(shards[27], "wa", axis=0, tiled=True),
-    )
-    tensor_bundle = shaped(gathered)
+    tensor_bundle = gather_weights(shards)
     small = [
         tensor_bundle[number].astype(jnp.float32)
         for number in (0, 1, 2, 7, 10, 13, 18, 19, 20, 21, 22, 23, 24, 25)
@@ -508,31 +477,15 @@
         speed_weighted_lookup,
     )
     head_count = model_width // HEAD_SIZE
-    identity = jnp.broadcast_to(
-        jnp.eye(HEAD_SIZE, dtype=jnp.float32), (head_count, HEAD_SIZE, HEAD_SIZE)
-    )
-    zero_state = jnp.zeros((head_count, HEAD_SIZE, HEAD_SIZE), jnp.float32)
-    block_len = math.gcd(length, 32)
-    block_count = length // block_len
-
-    def fold(tensor_entry):
-        return tensor_entry.reshape((block_count, block_len) + tensor_entry.shape[1:])
-
-    folded = tuple((fold(tensor_entry) for tensor_entry in readied_arguments))
-    keep_folded = fold(keeping)
-    span_maps, span_shifts, local_out, carried = jax.vmap(span_sweep)(folded, keep_folded)
-    (block_map, block_shift), (start_map, start_shift) = lax.scan(
-        prefix_step, (identity, zero_state), (span_maps, span_shifts)
-    )
-    prior_map, prior_state = entering(
-        (block_map, block_shift), "sa", chain_join, (identity, zero_state), False
-    )
-    start_states = (
-        jnp.einsum("hij,khjl->khil", prior_state, start_map, precision=HIGHEST) + start_shift
-    )
-    unit_outcomes = (
-        local_out + jnp.einsum("khij,klhj->klhi", start_states, carried, precision=HIGHEST)
-    ).reshape((length, head_count, HEAD_SIZE))
+
+    def sweep(*parts):
+        return block_sweep(*parts, keeping)
+
+    (block_map, block_shift, local_out, carried), sweep_back = jax.vjp(sweep, *readied_arguments)
+    block_maps, start_state = chain_states(block_map, block_shift, "sa")
+    unit_outcomes = jnp.swapaxes(
+        local_out + jnp.einsum("htj,hij->hti", carried, start_state, precision=HIGHEST), 0, 1
+    )
     blended_outcome, finish_back = jax.vjp(
         complete_unit,
         unit_outcomes,
@@ -556,37 +509,7 @@
     pre_act = matrix_multiply(channel_low, latent_entry_array)
     hidden_low = jnp.square(jax.nn.relu(pre_act)).astype(jnp.bfloat16)
     block_out = residual_mid + matrix_multiply(hidden_low, latent_exit_array)
-    regathered = (
-        lax.all_gather(shards[0], "wa", axis=0, tiled=True),
-        lax.all_gather(shards[1], "wa", axis=0, tiled=True),
-        lax.all_gather(shards[2], "wa", axis=0, tiled=True),
-        lax.all_gather(shards[3], "wa", axis=0, tiled=True),
-        lax.all_gather(shards[4], "wa", axis=0, tiled=True),
-        lax.all_gather(shards[5], "wa", axis=0, tiled=True),
-        lax.all_gather(shards[6], "wa", axis=0, tiled=True),
-        lax.all_gather(shards[7], "wa", axis=0, tiled=True),
-        lax.all_gather(shards[8], "wa", axis=0, tiled=True),
-        lax.all_gather(shards[9], "wa", axis=0, tiled=True),
-        lax.all_gather(shards[10], "wa", axis=0, tiled=True),
-        lax.all_gather(shards[11], "wa", axis=0, tiled=True),
-        lax.all_gather(shards[12], "wa", axis=0, tiled=True),
-        lax.all_gather(shards[13], "wa", axis=0, tiled=True),
-        lax.all_gather(shards[14], "wa", axis=0, tiled=True),
-        lax.all_gather(shards[15], "wa", axis=0, tiled=True),
-        lax.all_gather(shards[16], "wa", axis=0, tiled=True),
-        lax.all_gather(shards[17], "wa", axis=0, tiled=True),
-        lax.all_gather(shards[18], "wa", axis=0, tiled=True),
-        lax.all_gather(shards[19], "wa", axis=0, tiled=True),
-        lax.all_gather(shards[20], "wa", axis=0, tiled=True),
-        lax.all_gather(shards[21], "wa", axis=0, tiled=True),
-        lax.all_gather(shards[22], "wa", axis=0, tiled=True),
-        lax.all_gather(shards[23], "wa", axis=0, tiled=True),
-        lax.all_gather(shards[24], "wa", axis=0, tiled=True),
-        lax.all_gather(shards[25], "wa", axis=0, tiled=True),
-        lax.all_gather(shards[26], "wa", axis=0, tiled=True),
-        lax.all_gather(shards[27], "wa", axis=0, tiled=True),
-    )
-    back_weights = matrices(shaped(regathered))
+    back_weights = matrices(tensor_bundle)
     (
         back_receptance,
         back_key,
@@ -630,16 +553,16 @@
         grad_lnx_bias,
         present_token_boost_slope,
     ) = finish_back(grad_mixed)
-    grad_folded = fold(grad_outputs)
-    span_grads = jnp.einsum("klhi,klhj->khij", grad_folded, carried, precision=HIGHEST)
-    local_grad, unused_ends = lax.scan(back_step, zero_state, (span_maps, span_grads), reverse=True)
-    later_map, later_grad = entering(
-        (jnp.swapaxes(block_map, 1, 2), local_grad), "sa", chain_join, (identity, zero_state), True
-    )
-    unused_start, end_grads = lax.scan(back_step, later_grad, (span_maps, span_grads), reverse=True)
-    state_grads = jax.vmap(span_back)(start_states, folded, keep_folded, grad_folded, end_grads)
-    state_grads = tuple(
-        (tensor_entry.reshape((length, head_count, HEAD_SIZE)) for tensor_entry in state_grads)
+    grad_heads = jnp.swapaxes(grad_outputs, 0, 1)
+    local_grad = jnp.einsum("hti,htj->hij", grad_heads, carried, precision=HIGHEST)
+    end_grad = chain_grads(block_maps, local_grad, "sa")
+    state_grads = sweep_back(
+        (
+            jnp.einsum("hij,hil->hjl", start_state, end_grad, precision=HIGHEST),
+            end_grad,
+            grad_heads,
+            jnp.einsum("hti,hij->htj", grad_heads, start_state, precision=HIGHEST),
+        )
     )
     prep_grads = (
         state_grads[0] + grad_recept_a,
@@ -715,45 +638,41 @@
     )
     grad_input, grad_ln1_gain, grad_ln1_bias = ln_one_back(grad_normed_one)
     grad_input = grad_input + grad_mid
-    flat_grads = tuple(
-        (
-            tensor_entry.reshape(-1)
-            for tensor_entry in (
-                grad_ln1_gain,
-                grad_ln1_bias,
-                grad_mix_time,
-                grad_w_receptance,
-                grad_w_key,
-                grad_w_value,
-                grad_w_output,
-                grad_decay_base,
-                grad_decay_down,
-                decay_second_factor_gradient,
-                grad_rate_base,
-                grad_rate_down,
-                rate_second_factor_gradient,
-                value_residual_logits_gradient,
-                value_residual_first_gradient,
-                value_residual_second_gradient,
-                grad_gate_down,
-                grad_gate_up,
-                grad_key_norm,
-                grad_key_rate,
-                present_token_boost_slope,
-                grad_lnx_gain,
-                grad_lnx_bias,
-                grad_ln2_gain,
-                grad_ln2_bias,
-                grad_mix_channel,
-                grad_ffn_key,
-                grad_ffn_value,
-            )
-        )
-    )
-    owned = lax.psum_scatter(flat_grads, "wa", scatter_dimension=0, tiled=True)
-    summed = tuple(
-        jax.tree.map(lambda part: part.astype(jnp.float32), lax.psum(shortened(owned), "sa"))
-    )
+    grads = (
+        grad_ln1_gain,
+        grad_ln1_bias,
+        grad_mix_time,
+        grad_w_receptance,
+        grad_w_key,
+        grad_w_value,
+        grad_w_output,
+        grad_decay_base,
+        grad_decay_down,
+        decay_second_factor_gradient,
+        grad_rate_base,
+        grad_rate_down,
+        rate_second_factor_gradient,
+        value_residual_logits_gradient,
+        value_residual_first_gradient,
+        value_residual_second_gradient,
+        grad_gate_down,
+        grad_gate_up,
+        grad_key_norm,
+        grad_key_rate,
+        present_token_boost_slope,
+        grad_lnx_gain,
+        grad_lnx_bias,
+        grad_ln2_gain,
+        grad_ln2_bias,
+        grad_mix_channel,
+        grad_ffn_key,
+        grad_ffn_value,
+    )
+    small_places = [i for i in range(len(grads)) if i not in BIG]
+    summed = dict(zip(small_places, reduce_small([grads[i] for i in small_places])))
+    for i in BIG:
+        summed[i] = reduce_big(grads[i])
+    summed = tuple((summed[i] for i in range(len(grads))))
     return (block_out.astype(jnp.bfloat16), grad_input, grad_first) + summed
 
 

time: 4940 us -> 1410 us (0.29)
  blocking collectives: 2570 us -> 11.3 us
  other arithmetic: 1100 us -> 58.1 us
  waiting for transfers between devices: 62.3 us -> 1020 us
  local copies, waits for them, and re-layouts: 970 us -> 123 us
    unnamed x1 -> x0, blocking collectives: 2020 us -> none
    mul x97 -> x5, other arithmetic: 613 us -> 5.87 us  [the longest x3 3.65 us: block_sweep(): end_decay = reached[-1, 0] * jnp.exp(total[:, -1])]
    all_gather x26 -> x1, blocking collectives: 556 us -> 11.3 us  [chain_grads(): lax.all_gather(local_grad.astype(jnp.bfloat16), axis).astype(jnp.float32)]
    reduce_scatter x0 -> x7, waiting for transfers between devices: none -> 518 us  [the longest x6 454 us: reduce_big(): lax.psum_scatter(grad.astype(jnp.bfloat16), 'wa', scatter_dimension=0, ti...]
    all_gather x6 -> x8, waiting for transfers between devices: 0.03 us -> 435 us  [the longest x6 391 us: gather_weights(): lax.all_gather(shards[i].reshape(-1, shapes[i][1]), 'wa', axis=0, tiled=T...]
    reduce_sum x97 -> x5, other arithmetic: 314 us -> 4.28 us  [the longest x1 2.11 us: complete_unit(): acceptor_lines * lagged_lookup_entry]
    mul x646 -> x5, local copies, waits for them, and re-layouts: 303 us -> 5.54 us  [the longest x2 2.28 us: prepare_inputs(): -DECAY_FACTOR * jax.nn.sigmoid(fading_feature_odds + decay_lowrank_output)]
    while x676 -> x0, local copies, waits for them, and re-layouts: 168 us -> none
  transfers between devices with their start and end apart: 13 -> 21, of which waited for: 2 -> 17; matrix products, arithmetic and copies ran while one was open for 28% -> 15% of each run, Pallas kernels for 0% -> 0%
where the time goes in v1:
time: 1410 us; the launch traced here: 1400 us
  waiting for transfers between devices  1020 us (72%)
  matrix products  153 us (11%)
  local copies, waits for them, and re-layouts  123 us (9%)
  other arithmetic  58.1 us (4%)
  between operations  19.7 us (1%)
    reduce_scatter x6, waiting for transfers between devices, reduce_big(): lax.psum_scatter(grad.astype(jnp.bfloat16), 'wa', scatter_dimension=0, ti...  454 us
    all_gather x6, waiting for transfers between devices, gather_weights(): lax.all_gather(shards[i].reshape(-1, shapes[i][1]), 'wa', axis=0, tiled=T...  391 us
    psum x1, waiting for transfers between devices, reduce_small(): total = lax.psum(part, 'sa').reshape(-1).astype(jnp.float32)  69.4 us
    reduce_scatter x1, waiting for transfers between devices, reduce_small(): lax.psum_scatter(packed.reshape(-1, 128), 'wa', scatter_dimension=0, tile...  64.5 us
    unnamed x542, local copies, waits for them, and re-layouts  48.9 us
    dot_general x31, matrix products, batched(): return jnp.einsum(spec, left, right, precision=MATRIX_PRECISION)  48.5 us
    all_gather x1, waiting for transfers between devices, gather_weights(): packed = lax.all_gather(jnp.concatenate([shards[i] for i in small]), 'wa')  43.2 us
    dot_general x14, matrix products, matrix_product_pullback(): lax.dot_general(left_low, grad_low, (((0,), (0,)), ((), ())), preferred_e...  34.4 us
  transfers between devices with their start and end apart: 21, of which 17 were waited for; matrix products, arithmetic and copies ran while one was open for 15% of the time, Pallas kernels for 0%

profile of v1, /device:TPU:0, one launch (start us, length us, event | category | flops | bytes accessed | tf_op | source)
XLA Modules:
  0.0 1400.0 jit_solution(12058227078617959396)
XLA Ops:
  32.3 3.3 collective-permute-start
  43.4 43.2 %all-gather.26.cloned.1.call-done = bf16[8,1,84352]{2,1,0:T(2,128)(2,1)} async-done(((bf16[1,1,84352]{2,1,0:T(2,128)(2,1)}), bf16[8,1,84352]{2,1,0:T(2,128)(2,1)}) %all-gather.26.cloned.1.call-update) | async-done | bytes 1349648 | tf_op jit(solution)/shard_map/all_gather | solution.py:60
  103.3 33.8 %all-gather.12.cloned.1.call-done = bf16[1024,1024]{1,0:T(8,128)(2,1)} async-done(((bf16[128,1024]{1,0:T(8,128)(2,1)}), bf16[1024,1024]{1,0:T(8,128)(2,1)}) %all-gather.12.cloned.1.call-update) | async-done | bytes 2097168 | tf_op jit(solution)/shard_map/all_gather | solution.py:68
  137.2 3.1 broadcast_multiply_fusion.2
  140.5 47.2 %all-gather.14.cloned.1.call-done = bf16[1024,1024]{1,0:T(8,128)(2,1)} async-done(((bf16[128,1024]{1,0:T(8,128)(2,1)}), bf16[1024,1024]{1,0:T(8,128)(2,1)}) %all-gather.14.cloned.1.call-update) | async-done | bytes 2097168 | tf_op jit(solution)/shard_map/all_gather | solution.py:68
  187.7 2.1 fusion.270
  192.9 2.2 fusion.137
  206.6 31.5 %all-gather.16.cloned.1.call-done = bf16[1024,1024]{1,0:T(8,128)(2,1)} async-done(((bf16[128,1024]{1,0:T(8,128)(2,1)}), bf16[1024,1024]{1,0:T(8,128)(2,1)}) %all-gather.16.cloned.1.call-update) | async-done | bytes 2097168 | tf_op jit(solution)/shard_map/all_gather | solution.py:68
  238.1 2.9 multiply_add_fusion.4
  241.2 2.4 fusion.53
  243.6 2.6 fusion.36
  252.7 2.3 reshape.678
  255.0 2.3 reshape.679
  259.9 2.2 reshape.676
  262.1 2.4 reshape.675
  267.8 2.3 fusion.52
  278.4 2.4 fusion.266
  282.2 2.3 multiply_convert_fusion.2
  284.4 38.9 %all-gather.20.cloned.1.call-done = bf16[1024,1024]{1,0:T(8,128)(2,1)} async-done(((bf16[128,1024]{1,0:T(8,128)(2,1)}), bf16[1024,1024]{1,0:T(8,128)(2,1)}) %all-gather.20.cloned.1.call-update) | async-done | bytes 2097168 | tf_op jit(solution)/shard_map/all_gather | solution.py:68
  323.3 2.1 fusion.267
  329.4 119.5 %all-gather.22.cloned.1.call-done = bf16[1024,4096]{1,0:T(8,128)(2,1)} async-done(((bf16[128,4096]{1,0:T(8,128)(2,1)}), bf16[1024,4096]{1,0:T(8,128)(2,1)}) %all-gather.22.cloned.1.call-update) | async-done | bytes 8388624 | tf_op jit(solution)/shard_map/all_gather | solution.py:68
  448.9 4.8 convolution_maximum_fusion
  453.7 120.5 %all-gather.24.cloned.1.call-done = bf16[4096,1024]{1,0:T(8,128)(2,1)} async-done(((bf16[512,1024]{1,0:T(8,128)(2,1)}), bf16[4096,1024]{1,0:T(8,128)(2,1)}) %all-gather.24.cloned.1.call-update) | async-done | bytes 8388624 | tf_op jit(solution)/shard_map/all_gather | solution.py:68
  574.2 6.5 fusion.1
  580.7 4.3 multiply_reduce_fusion
  589.8 2.3 multiply_reduce_fusion.1
  593.5 2.2 fusion.252
  606.6 11.3 all-gather.1
  617.9 2.3 copy.255
  628.1 2.4 convolution_add_fusion
  637.6 2.1 convolution_select_fusion.2
  643.1 4.0 fusion.3
  647.4 2.6 fusion.2
  650.3 2.4 bitcast_multiply_fusion.1
  652.7 2.1 multiply_reduce_fusion.13
  655.5 2.1 convolution_convert_fusion.5
  657.7 2.0 copy.265
  660.4 2.1 add_add_fusion.1
  662.5 2.1 copy.272
  666.7 3.3 multiply_reduce_fusion.4
  670.7 2.1 convolution_convert_fusion.4
  676.7 2.6 fusion.8
  681.4 3.2 fusion.254
  687.4 3.2 convolution_convert_fusion.2
  690.6 6.9 convolution_convert_fusion.1
  697.8 6.7 convolution_convert_fusion
  710.4 6.1 fusion.18
  716.5 2.1 copy.275
  734.8 2.0 copy.281
  736.9 2.1 multiply_reduce_fusion.3
  761.9 2.6 reshape.700
  764.5 2.2 reshape.701
  766.9 2.5 fusion.253
  772.7 3.2 reshape.702
  777.7 16.7 %reduce-scatter.12.cloned.1.call-done = bf16[128,1024]{1,0:T(8,128)(2,1)} async-done(((bf16[1024,1024]{1,0:T(8,128)(2,1)}), bf16[128,1024]{1,0:T(8,128)(2,1)}) %reduce-scatter.12.cloned.1.call-update) | async-done | bytes 262160 | tf_op jit(solution)/shard_map/reduce_scatter | solution.py:73
  796.1 68.6 %reduce-scatter.14.cloned.1.call-done = bf16[128,1024]{1,0:T(8,128)(2,1)} async-done(((bf16[1024,1024]{1,0:T(8,128)(2,1)}), bf16[128,1024]{1,0:T(8,128)(2,1)}) %reduce-scatter.14.cloned.1.call-update) | async-done | bytes 262160 | tf_op jit(solution)/shard_map/reduce_scatter | solution.py:73
  866.5 68.6 %reduce-scatter.16.cloned.1.call-done = bf16[128,1024]{1,0:T(8,128)(2,1)} async-done(((bf16[1024,1024]{1,0:T(8,128)(2,1)}), bf16[128,1024]{1,0:T(8,128)(2,1)}) %reduce-scatter.16.cloned.1.call-update) | async-done | bytes 262160 | tf_op jit(solution)/shard_map/reduce_scatter | solution.py:73
  936.8 150.0 %reduce-scatter.18.cloned.1.call-done = bf16[128,4096]{1,0:T(8,128)(2,1)} async-done(((bf16[1024,4096]{1,0:T(8,128)(2,1)}), bf16[128,4096]{1,0:T(8,128)(2,1)}) %reduce-scatter.18.cloned.1.call-update) | async-done | bytes 1048592 | tf_op jit(solution)/shard_map/reduce_scatter | solution.py:73
  1086.8 2.4 copy.300
  1089.3 149.5 %reduce-scatter.20.cloned.1.call-done = bf16[512,1024]{1,0:T(8,128)(2,1)} async-done(((bf16[4096,1024]{1,0:T(8,128)(2,1)}), bf16[512,1024]{1,0:T(8,128)(2,1)}) %reduce-scatter.20.cloned.1.call-update) | async-done | bytes 1048592 | tf_op jit(solution)/shard_map/reduce_scatter | solution.py:73
  1238.8 2.5 copy.301
  1241.2 64.5 %reduce-scatter.8.cloned.1.call-done = bf16[672,128]{1,0:T(8,128)(2,1)} async-done(((bf16[5376,128]{1,0:T(8,128)(2,1)}), bf16[672,128]{1,0:T(8,128)(2,1)}) %reduce-scatter.8.cloned.1.call-update) | async-done | bytes 172048 | tf_op jit(solution)/shard_map/reduce_scatter | solution.py:83
  1305.9 5.4 fusion.27
  1312.5 69.4 %all-reduce.24.cloned.1.call-done = (bf16[672,128]{1,0:T(8,128)(2,1)}, bf16[131072]{0:T(1024)(128)(2,1)}, bf16[131072]{0:T(1024)(128)(2,1)}, bf16[131072]{0:T(10...) async-done(((bf16[672,128]{1,0:T(8,128)(2,1)}, bf16[131072]{0:T(1024)(128)(2,1)}, bf16[131072]{0:T(1024)(128)(2,1)}, ...) | async-done | bytes 3317776 | tf_op jit(solution)/shard_map/psum | solution.py:84
  (779 shorter events, 202.7 us)
Async XLA Ops:
  7.2 22.9 %copy-start.139 = (bf16[131072]{0:T(1024)(128)(2,1)S(1)}, bf16[131072]{0:T(1024)(128)(2,1)}, u32[]{:S(2)}) copy-start(bf16[131072]{0:T(1024)(128)(2,1)} %param.39) | copy-start | bytes 786436
  7.2 23.8 %copy-start.238 = (s32[128]{0:T(128)S(1)}, s32[128]{0:T(128)}, u32[]{:S(2)}) copy-start(s32[128]{0:T(128)} %param.34) | copy-start | bytes 1540
  7.2 28.4 %copy-start.140 = (bf16[131072]{0:T(1024)(128)(2,1)S(1)}, bf16[131072]{0:T(1024)(128)(2,1)}, u32[]{:S(2)}) copy-start(bf16[131072]{0:T(1024)(128)(2,1)} %param.41) | copy-start | bytes 786436
  7.2 30.1 %copy-start.10 = (bf16[128,1024]{1,0:T(8,128)(2,1)S(1)}, bf16[128,1024]{1,0:T(8,128)(2,1)}, u32[]{:S(2)}) copy-start(bf16[128,1024]{1,0:T(8,128)(2,1)} %param.32) | copy-start | bytes 786436
  7.2 79.3 %all-gather.26.cloned.1.call-start = ((), (), s32[]{:S(2)}) async-start(), calls=%async_computation.21 | async-start | bytes 3036672 | tf_op jit(solution)/shard_map/all_gather | solution.py:60
  28.2 108.9 %all-gather.12.cloned.1.call-start = ((), (), s32[]{:S(2)}) async-start(), calls=%async_computation.7 | async-start | bytes 2359296 | tf_op jit(solution)/shard_map/all_gather | solution.py:68
  30.1 157.6 %all-gather.14.cloned.1.call-start = ((), (), s32[]{:S(2)}) async-start(), calls=%async_computation.8 | async-start | bytes 2359296 | tf_op jit(solution)/shard_map/all_gather | solution.py:68
  31.0 207.1 %all-gather.16.cloned.1.call-start = ((), (), s32[]{:S(2)}) async-start(), calls=%async_computation.9 | async-start | bytes 2359296 | tf_op jit(solution)/shard_map/all_gather | solution.py:68
  32.3 7.9 collective-permute-start
  36.4 235.6 %all-gather.18.cloned.1.call-start = ((), (), s32[]{:S(2)}) async-start(), calls=%async_computation.10 | async-start | bytes 2621440 | tf_op jit(solution)/shard_map/all_gather | solution.py:34
  37.4 57.3 %copy-start.193 = (f32[128]{0:T(128)}, f32[128]{0:T(128)S(1)}, u32[]{:S(2)}) copy-start(f32[128]{0:T(128)S(1)} %broadcast_multiply_fusion.5) | copy-start | bytes 1540
  37.7 50.8 %copy-start.241 = (f32[128]{0:T(128)}, f32[128]{0:T(128)S(1)}, u32[]{:S(2)}) copy-start(f32[128]{0:T(128)S(1)} %fusion.66) | copy-start | bytes 1540
  37.7 57.1 %copy-start.216 = (f32[128]{0:T(128)}, f32[128]{0:T(128)S(1)}, u32[]{:S(2)}) copy-start(f32[128]{0:T(128)S(1)} %fusion.220) | copy-start | bytes 1540
  40.9 52.8 %copy-start.210 = (f32[128]{0:T(128)}, f32[128]{0:T(128)S(1)}, u32[]{:S(2)}) copy-start(f32[128]{0:T(128)S(1)} %get-tuple-element.82) | copy-start | bytes 1540
  42.8 46.4 %copy-start.221 = (f32[128]{0:T(128)}, f32[128]{0:T(128)S(1)}, u32[]{:S(2)}) copy-start(f32[128]{0:T(128)S(1)} %get-tuple-element.167) | copy-start | bytes 1540
  89.9 3.8 collective-permute-start.1
  97.8 95.1 %copy-start.27 = (f32[128,1024]{0,1:T(8,128)}, f32[128,1024]{0,1:T(8,128)S(1)}, u32[]{:S(2)}) copy-start(f32[128,1024]{0,1:T(8,128)S(1)} %copy.243) | copy-start | bytes 1572868
  100.0 37.2 %copy-start.55 = (f32[128,1024]{1,0:T(8,128)}, f32[128,1024]{1,0:T(8,128)S(1)}, u32[]{:S(2)}) copy-start(f32[128,1024]{1,0:T(8,128)S(1)} %fusion.22) | copy-start | bytes 1572868
  100.2 92.7 %copy-start.43 = (f32[128,1024]{0,1:T(8,128)}, f32[128,1024]{0,1:T(8,128)S(1)}, u32[]{:S(2)}) copy-start(f32[128,1024]{0,1:T(8,128)S(1)} %copy.246) | copy-start | bytes 1572868
  100.2 37.0 %copy-start.90 = (bf16[128,1024]{1,0:T(8,128)(2,1)S(1)}, bf16[128,1024]{1,0:T(8,128)(2,1)}, u32[]{:S(2)}) copy-start(bf16[128,1024]{1,0:T(8,128)(2,1)} %get-tuple-element.122) | copy-start | bytes 786436
  100.5 36.7 %copy-start.192 = (bf16[128,32]{0,1:T(8,128)(2,1)}, bf16[128,32]{0,1:T(8,128)(2,1)S(1)}, u32[]{:S(2)}) copy-start(bf16[128,32]{0,1:T(8,128)(2,1)S(1)} %convolution_convert_fusion.18) | copy-start | bytes 24580
  140.3 47.4 %copy-start.51 = (f32[128,1024]{1,0:T(8,128)}, f32[128,1024]{1,0:T(8,128)S(1)}, u32[]{:S(2)}) copy-start(f32[128,1024]{1,0:T(8,128)S(1)} %get-tuple-element.131) | copy-start | bytes 1572868
  140.5 125.5 %copy-start.5 = (f32[128,1024]{0,1:T(8,128)}, f32[128,1024]{0,1:T(8,128)S(1)}, u32[]{:S(2)}) copy-start(f32[128,1024]{0,1:T(8,128)S(1)} %copy.245) | copy-start | bytes 1572868
  190.6 79.4 %copy-start.17 = (f32[128,1024]{0,1:T(8,128)}, f32[128,1024]{0,1:T(8,128)S(1)}, u32[]{:S(2)}) copy-start(f32[128,1024]{0,1:T(8,128)S(1)} %copy.244) | copy-start | bytes 1572868
  205.0 33.1 %copy-start.39 = (bf16[128,1024]{1,0:T(8,128)(2,1)S(1)}, bf16[128,1024]{1,0:T(8,128)(2,1)}, u32[]{:S(2)}) copy-start(bf16[128,1024]{1,0:T(8,128)(2,1)} %copy-done.38) | copy-start | bytes 786436
  205.0 33.1 %copy-start.123 = (bf16[128,1024]{1,0:T(8,128)(2,1)S(1)}, bf16[128,1024]{1,0:T(8,128)(2,1)}, u32[]{:S(2)}) copy-start(bf16[128,1024]{1,0:T(8,128)(2,1)} %param.33) | copy-start | bytes 786436
  246.3 21.5 %copy-start.2 = (f32[16,128,128]{2,1,0:T(8,128)}, f32[16,128,128]{2,1,0:T(8,128)S(1)}, u32[]{:S(2)}) copy-start(f32[16,128,128]{2,1,0:T(8,128)S(1)} %fusion.36) | copy-start | bytes 3145732
  250.8 72.6 %all-gather.20.cloned.1.call-start = ((), (), s32[]{:S(2)}) async-start(), calls=%async_computation.11 | async-start | bytes 2359296 | tf_op jit(solution)/shard_map/all_gather | solution.py:68
  252.6 196.3 %all-gather.22.cloned.1.call-start = ((), (), s32[]{:S(2)}) async-start(), calls=%async_computation.12 | async-start | bytes 9437184 | tf_op jit(solution)/shard_map/all_gather | solution.py:68
  255.0 319.2 %all-gather.24.cloned.1.call-start = ((), (), s32[]{:S(2)}) async-start(), calls=%async_computation.13 | async-start | bytes 9437184 | tf_op jit(solution)/shard_map/all_gather | solution.py:68
  257.4 518.6 %reduce-scatter.10.cloned.1.call-start = ((), (), s32[]{:S(2)}) async-start(), calls=%async_computation.15 | async-start | bytes 2359296 | tf_op jit(solution)/shard_map/reduce_scatter | solution.py:73
  257.9 8.2 copy-start.151
  281.8 43.6 %copy-start.65 = (f32[128,1024]{1,0:T(8,128)}, f32[128,1024]{1,0:T(8,128)S(1)}, u32[]{:S(2)}) copy-start(f32[128,1024]{1,0:T(8,128)S(1)} %copy.252) | copy-start | bytes 1572868
  284.4 41.5 %copy-start.92 = (bf16[128,1024]{1,0:T(8,128)(2,1)}, bf16[128,1024]{1,0:T(8,128)(2,1)S(1)}, u32[]{:S(2)}) copy-start(bf16[128,1024]{1,0:T(8,128)(2,1)S(1)} %get-tuple-element.75) | copy-start | bytes 786436
  284.4 41.3 %copy-start.188 = (f32[1024]{0:T(1024)S(1)}, f32[1024]{0:T(1024)}, u32[]{:S(2)}) copy-start(f32[1024]{0:T(1024)} %get-tuple-element.92) | copy-start | bytes 12292
  326.2 2.1 collective-permute-start.2
  586.4 3.4 collective-permute-start.3
  657.6 136.8 %reduce-scatter.12.cloned.1.call-start = ((), (), s32[]{:S(2)}) async-start(), calls=%async_computation.16 | async-start | bytes 2359296 | tf_op jit(solution)/shard_map/reduce_scatter | solution.py:73
  672.8 192.0 %reduce-scatter.14.cloned.1.call-start = ((), (), s32[]{:S(2)}) async-start(), calls=%async_computation.17 | async-start | bytes 2359296 | tf_op jit(solution)/shard_map/reduce_scatter | solution.py:73
  687.3 247.8 %reduce-scatter.16.cloned.1.call-start = ((), (), s32[]{:S(2)}) async-start(), calls=%async_computation.18 | async-start | bytes 2359296 | tf_op jit(solution)/shard_map/reduce_scatter | solution.py:73
  690.6 396.3 %reduce-scatter.18.cloned.1.call-start = ((), (), s32[]{:S(2)}) async-start(), calls=%async_computation.19 | async-start | bytes 9437184 | tf_op jit(solution)/shard_map/reduce_scatter | solution.py:73
  697.6 541.2 %reduce-scatter.20.cloned.1.call-start = ((), (), s32[]{:S(2)}) async-start(), calls=%async_computation.20 | async-start | bytes 9437184 | tf_op jit(solution)/shard_map/reduce_scatter | solution.py:73
  704.5 601.2 %reduce-scatter.8.cloned.1.call-start = ((), (), s32[]{:S(2)}) async-start(), calls=%async_computation.14 | async-start | bytes 1548288 | tf_op jit(solution)/shard_map/reduce_scatter | solution.py:83
  732.5 34.2 %collective-permute-start.4 = (f32[1,1024]{1,0:T(1,128)}, f32[1,1024]{1,0:T(1,128)}, u32[]{:S(2)}, u32[]{:S(2)}) collective-permute-start(f32[1,1024]{1,0:T(1,128)} %split.49), channel_id=1, source_target_pairs={{1,0},{2,1},{3,2},{5,4},{6,5},{7,6},{9,8},{10,9},{11,10},{13,12},{... | collective-permute-start | bytes 12296 | tf_op jit(solution)/shard_map/ppermute | solution.py:25
  736.9 10.9 copy-start.89
  736.9 10.9 copy-start.134
  736.9 11.7 copy-start.80
  736.9 12.7 copy-start.103
  739.0 11.5 copy-start.203
  739.0 11.5 copy-start.204
  739.0 11.5 copy-start.205
  739.0 11.5 copy-start.206
  739.0 11.5 copy-start.207
  739.0 11.5 copy-start.208
  739.0 11.5 copy-start.105
  755.0 11.7 copy-start.163
  755.0 11.7 copy-start.166
  758.4 8.3 copy-start.169
  758.4 8.3 copy-start.172
  758.4 8.3 copy-start.175
  758.4 8.3 copy-start.194
  775.9 606.0 %all-reduce.24.cloned.1.call-start = ((), (), s32[]{:S(2)}) async-start(), calls=%async_computation.22 | async-start | bytes 6635520 | tf_op jit(solution)/shard_map/psum | solution.py:84
  1241.2 64.6 %copy-start.9 = (f32[128,1024]{1,0:T(8,128)S(1)}, f32[128,1024]{1,0:T(8,128)}, u32[]{:S(2)}) copy-start(f32[128,1024]{1,0:T(8,128)} %copy-done.7) | copy-start | bytes 1572868
  1381.9 8.5 copy-start.120
  (203 other events, 645.8 us)
Sparse Core Ops, SparseCore 0:
  28.4 58.1 all-gather.25
  89.3 47.8 all-gather.11
  139.9 47.7 all-gather.13
  190.3 47.7 all-gather.15
  250.9 21.0 all-gather.17
  274.0 49.2 all-gather.19
  325.4 123.4 all-gather.21
  451.0 123.1 all-gather.23
  657.7 65.9 reduce-scatter.9
  727.6 66.7 reduce-scatter.11
  798.0 66.7 reduce-scatter.13
  868.1 66.9 reduce-scatter.15
  938.7 148.0 reduce-scatter.17
  1090.8 147.9 reduce-scatter.19
  1242.0 63.6 reduce-scatter.7
  1310.2 71.5 all-reduce.23

commit v2 on v1

--- a/solution.py
+++ b/solution.py
@@ -25,7 +25,8 @@
     return lax.ppermute(block, axis, route)
 
 
-BIG = (3, 4, 5, 6, 26, 27)
+SQUARE = (3, 4, 5, 6)
+BIG = SQUARE + (26, 27)
 
 
 def chain_states(block_map, block_shift, axis):
@@ -54,41 +55,35 @@
     return grad
 
 
+def small_rows(flat, rows):
+    flat = jnp.pad(flat, ((0, 0), (0, -flat.shape[1] % (rows * 128))))
+    return flat.reshape(flat.shape[0] * rows, -1)
+
+
 def gather_weights(shards):
     shapes = layout()
     small = [i for i in range(len(shards)) if i not in BIG]
-    packed = lax.all_gather(jnp.concatenate([shards[i] for i in small]), "wa")
+    squares = [shards[i].reshape(-1, shapes[i][1]) for i in SQUARE]
+    flat = small_rows(jnp.concatenate([shards[i] for i in small])[None], squares[0].shape[0])
+    packed = lax.all_gather(jnp.concatenate(squares + [flat], 1), "wa", axis=0, tiled=True)
     whole = [None] * len(shards)
+    at = 0
+    for i in SQUARE:
+        whole[i] = packed[:, at : at + shapes[i][1]]
+        at += shapes[i][1]
+    packed = packed[:, at:].reshape(lax.axis_size("wa"), -1)
     at = 0
     for i in small:
         n = shards[i].shape[0]
         whole[i] = packed[:, at : at + n].reshape(shapes[i])
         at += n
-    for i in BIG:
+    for i in (26, 27):
         whole[i] = lax.all_gather(shards[i].reshape(-1, shapes[i][1]), "wa", axis=0, tiled=True)
     return tuple(whole)
 
 
-def reduce_big(grad):
-    part = lax.psum_scatter(grad.astype(jnp.bfloat16), "wa", scatter_dimension=0, tiled=True)
-    return lax.psum(part, "sa").reshape(-1).astype(jnp.float32)
-
-
-def reduce_small(grads):
-    owners = lax.axis_size("wa")
-    packed = jnp.concatenate(
-        [grad.astype(jnp.bfloat16).reshape(owners, -1) for grad in grads], axis=1
-    )
-    packed = jnp.pad(packed, ((0, 0), (0, -packed.shape[1] % 2048)))
-    part = lax.psum_scatter(packed.reshape(-1, 128), "wa", scatter_dimension=0, tiled=True)
-    total = lax.psum(part, "sa").reshape(-1).astype(jnp.float32)
-    out = []
-    at = 0
-    for grad in grads:
-        n = grad.size // owners
-        out.append(total[at : at + n])
-        at += n
-    return out
+def scattered(grad):
+    return lax.psum_scatter(grad.astype(jnp.bfloat16), "wa", scatter_dimension=0, tiled=True)
 
 
 def layout():
@@ -482,6 +477,9 @@
         return block_sweep(*parts, keeping)
 
     (block_map, block_shift, local_out, carried), sweep_back = jax.vjp(sweep, *readied_arguments)
+    block_map, block_shift, latent_entry_array = lax.optimization_barrier(
+        (block_map, block_shift, latent_entry_array)
+    )
     block_maps, start_state = chain_states(block_map, block_shift, "sa")
     unit_outcomes = jnp.swapaxes(
         local_out + jnp.einsum("htj,hij->hti", carried, start_state, precision=HIGHEST), 0, 1
@@ -509,7 +507,7 @@
     pre_act = matrix_multiply(channel_low, latent_entry_array)
     hidden_low = jnp.square(jax.nn.relu(pre_act)).astype(jnp.bfloat16)
     block_out = residual_mid + matrix_multiply(hidden_low, latent_exit_array)
-    back_weights = matrices(tensor_bundle)
+    back_weights = matrices(tensor_bundle)[:-2] + (latent_entry_array, latent_exit_array)
     (
         back_receptance,
         back_key,
@@ -564,6 +562,8 @@
             jnp.einsum("hti,hij->htj", grad_heads, start_state, precision=HIGHEST),
         )
     )
+    state_grads, value_part = lax.optimization_barrier((state_grads, scattered(grad_ffn_value)))
+    key_part = scattered(grad_ffn_key)
     prep_grads = (
         state_grads[0] + grad_recept_a,
         state_grads[1],
@@ -668,10 +668,30 @@
         grad_ffn_key,
         grad_ffn_value,
     )
+    owners = lax.axis_size("wa")
     small_places = [i for i in range(len(grads)) if i not in BIG]
-    summed = dict(zip(small_places, reduce_small([grads[i] for i in small_places])))
-    for i in BIG:
-        summed[i] = reduce_big(grads[i])
+    low = [grad.astype(jnp.bfloat16) for grad in grads]
+    flat = jnp.concatenate([low[i].reshape(owners, -1) for i in small_places], axis=1)
+    packed = jnp.concatenate(
+        [low[i] for i in SQUARE] + [small_rows(flat, model_width // owners)], axis=1
+    )
+    packed, key_part = lax.optimization_barrier((packed, key_part))
+    packed, key_part, value_part = lax.psum((scattered(packed), key_part, value_part), "sa")
+    packed = packed.astype(jnp.float32)
+    summed = {
+        26: key_part.reshape(-1).astype(jnp.float32),
+        27: value_part.reshape(-1).astype(jnp.float32),
+    }
+    at = 0
+    for i in SQUARE:
+        summed[i] = packed[:, at : at + model_width].reshape(-1)
+        at += model_width
+    packed = packed[:, at:].reshape(-1)
+    at = 0
+    for i in small_places:
+        n = grads[i].size // owners
+        summed[i] = packed[at : at + n]
+        at += n
     summed = tuple((summed[i] for i in range(len(grads))))
     return (block_out.astype(jnp.bfloat16), grad_input, grad_first) + summed
 

time: 1410 us -> 1040 us (0.74)
  waiting for transfers between devices: 1020 us -> 647 us
    reduce_scatter x7 -> x2, waiting for transfers between devices: 518 us -> 104 us  [scattered(): lax.psum_scatter(grad.astype(jnp.bfloat16), 'wa', scatter_dimension=0, ti...]
    all_gather x6 -> x2, waiting for transfers between devices: 391 us -> 172 us  [gather_weights(): lax.all_gather(shards[i].reshape(-1, shapes[i][1]), 'wa', axis=0, tiled=T...]
    unnamed x16 -> x9, waiting for transfers between devices: 0.26 us -> 166 us
    all_gather x1, waiting for transfers between devices: 43.2 us -> 134 us  [gather_weights(): lax.all_gather(jnp.concatenate(squares + [flat], 1), 'wa', axis=0, tiled=...]
    unnamed x542 -> x584, local copies, waits for them, and re-layouts: 48.9 us -> 44.5 us
  transfers between devices with their start and end apart: 21 -> 13, of which waited for: 17 -> 9; matrix products, arithmetic and copies ran while one was open for 15% -> 27% of each run, Pallas kernels for 0% -> 0%
where the time goes in v2:
time: 1040 us; the launch traced here: 1030 us
  waiting for transfers between devices  647 us (62%)
  matrix products  150 us (14%)
  local copies, waits for them, and re-layouts  130 us (12%)
  other arithmetic  56.8 us (5%)
  between operations  20.4 us (2%)
  blocking collectives  11.6 us (1%)
  starting transfers between devices  10.8 us (1%)
    all_gather x2, waiting for transfers between devices, gather_weights(): lax.all_gather(shards[i].reshape(-1, shapes[i][1]), 'wa', axis=0, tiled=T...  172 us
    unnamed x9, waiting for transfers between devices  166 us
    all_gather x1, waiting for transfers between devices, gather_weights(): lax.all_gather(jnp.concatenate(squares + [flat], 1), 'wa', axis=0, tiled=...  134 us
    reduce_scatter x2, waiting for transfers between devices, scattered(): lax.psum_scatter(grad.astype(jnp.bfloat16), 'wa', scatter_dimension=0, ti...  104 us
    psum x1, waiting for transfers between devices, body(): lax.psum((scattered(packed), key_part, value_part), 'sa')  64 us
    unnamed x584, local copies, waits for them, and re-layouts  44.5 us
    dot_general x31, matrix products, batched(): return jnp.einsum(spec, left, right, precision=MATRIX_PRECISION)  41 us
    dot_general x14, matrix products, matrix_product_pullback(): lax.dot_general(grad_low, right, (((1,), (1,)), ((), ())), preferred_elem...  34.4 us
  transfers between devices with their start and end apart: 13, of which 9 were waited for; matrix products, arithmetic and copies ran while one was open for 27% of the time, Pallas kernels for 0%

profile of v2, /device:TPU:0, one launch (start us, length us, event | category | flops | bytes accessed | tf_op | source)
XLA Modules:
  0.0 1025.9 jit_solution(11325933071338148227)
XLA Ops:
  21.4 3.3 collective-permute-start
  33.0 134.5 %all-gather.6.cloned.1.call-done = bf16[1024,4864]{1,0:T(8,128)(2,1)} async-done(((bf16[128,4864]{1,0:T(8,128)(2,1)}), bf16[1024,4864]{1,0:T(8,128)(2,1)}) %all-gather.6.cloned.1.call-update) | async-done | bytes 9961488 | tf_op jit(solution)/shard_map/all_gather | solution.py:68
  171.2 2.1 collective-permute-start.1
  183.7 3.1 broadcast_multiply_fusion.3
  187.5 2.2 fusion.14
  194.3 3.1 multiply_add_fusion.5
  217.8 75.5 %all-gather.8.cloned.1.call-done = bf16[1024,4096]{1,0:T(8,128)(2,1)} async-done(((bf16[128,4096]{1,0:T(8,128)(2,1)}), bf16[1024,4096]{1,0:T(8,128)(2,1)}) %all-gather.8.cloned.1.call-update) | async-done | bytes 8388624 | tf_op jit(solution)/shard_map/all_gather | solution.py:81
  295.2 2.1 copy.219
  297.3 2.3 reshape.666
  301.9 2.2 reshape.665
  304.2 2.4 reshape.664
  309.3 2.3 fusion.68
  312.7 5.5 all-gather.10.cloned.1.call-done
  318.2 2.0 convert_element_type.447
  324.6 2.4 fusion.285
  331.3 2.2 fusion.286
  334.3 2.1 collective-permute-start.2
  338.8 4.7 convolution_maximum_fusion
  343.6 5.7 convolution_convert_fusion.1
  349.5 96.2 %all-gather.12.cloned.1.call-done = bf16[4096,1024]{1,0:T(8,128)(2,1)} async-done(((bf16[512,1024]{1,0:T(8,128)(2,1)}), bf16[4096,1024]{1,0:T(8,128)(2,1)}) %all-gather.12.cloned.1.call-update) | async-done | bytes 8388624 | tf_op jit(solution)/shard_map/all_gather | solution.py:81
  445.7 6.4 fusion.1
  452.2 8.4 multiply_reduce_fusion
  463.3 5.6 convolution_convert_fusion
  471.0 2.4 multiply_reduce_fusion.1
  474.8 3.9 fusion.266
  480.3 2.0 copy.222
  486.9 11.6 %all-gather = bf16[64,64,64]{2,1,0:T(8,128)(2,1)} all-gather(bf16[16,64,64]{2,1,0:T(8,128)(2,1)S(1)} %convolution_convert_fusion.4), channel_id=2, replica_groups=mesh['wa'=8,'sa'=4] {'sa'}, dimensions={0}, use_global_device_ids=true | all-gather | bytes 655360 | tf_op jit(solution)/shard_map/all_gather | solution.py:48
  498.5 2.7 copy.225
  511.6 2.4 convolution_add_fusion
  520.4 2.6 fusion.2
  523.0 3.0 fusion.3
  527.7 2.1 copy.235
  533.7 4.5 add_bitcast_fusion
  540.9 2.1 fusion.161
  543.1 2.1 convolution_add_fusion.2
  545.2 2.6 fusion.21
  550.8 2.6 reshape.687
  553.4 2.2 reshape.688
  555.6 6.9 fusion.33
  562.5 33.9 %reduce-scatter.6.cloned.1.call-done = bf16[512,1024]{1,0:T(8,128)(2,1)} async-done(((bf16[4096,1024]{1,0:T(8,128)(2,1)}), bf16[512,1024]{1,0:T(8,128)(2,1)}) %reduce-scatter.6.cloned.1.call-update) | async-done | bytes 1048592 | tf_op jit(solution)/shard_map/reduce_scatter | solution.py:86
  598.6 2.0 fusion.189
  606.8 2.1 copy.236
  611.8 2.1 copy.242
  613.9 2.0 copy.237
  617.0 3.2 fusion.268
  621.9 2.5 fusion.8
  625.0 2.6 fusion.12
  627.8 2.7 fusion.16
  635.4 2.1 copy.249
  637.5 2.1 multiply_reduce_fusion.3
  646.4 2.1 convert_dynamic-update-slice_fusion.3
  648.5 2.1 convert_dynamic-update-slice_fusion.2
  650.6 2.1 convert_dynamic-update-slice_fusion.1
  652.7 2.1 convert_dynamic-update-slice_fusion
  664.4 2.5 fusion.267
  669.8 3.3 reshape.689
  673.1 2.6 copy.251
  675.7 2.8 constant_dynamic-update-slice_fusion.27
  678.5 69.9 %reduce-scatter.8.cloned.1.call-done = bf16[128,4096]{1,0:T(8,128)(2,1)} async-done(((bf16[1024,4096]{1,0:T(8,128)(2,1)}), bf16[128,4096]{1,0:T(8,128)(2,1)}) %reduce-scatter.8.cloned.1.call-update) | async-done | bytes 1048592 | tf_op jit(solution)/shard_map/reduce_scatter | solution.py:86
  748.4 13.2 %copy.269 = bf16[1024,4864]{1,0:T(8,128)(2,1)} copy(bf16[1024,4864]{0,1:T(8,128)(2,1)} %constant_dynamic-update-slice_fusion.27) | data formatting | bytes 19922944
  765.3 166.1 %reduce-scatter.10.cloned.1.call-done = bf16[128,4864]{1,0:T(8,128)(2,1)} async-done(((bf16[1024,4864]{1,0:T(8,128)(2,1)}), bf16[128,4864]{1,0:T(8,128)(2,1)}) %reduce-scatter.10.cloned.1.call-update) | async-done | bytes 1245200
  931.4 2.6 copy.270
  935.1 5.4 fusion.45
  941.7 64.0 %all-reduce.25.cloned.1.call-done = (bf16[128,4864]{0,1:T(8,128)(2,1)}, bf16[524288]{0:T(1024)(128)(2,1)}, bf16[524288]{0:T(1024)(128)(2,1)}) async-done(((bf16[128,4864]{0,1:T(8,128)(2,1)}, bf16[524288]{0:T(1024)(128)(2,1)}, bf16[524288]{0:T(1024)(128)(2,1)}), (bf16[128,4864]{0,1:T(8,128)(2,1)}, bf16[524288]{0:T(1024)(128)(2,1)}, bf16[524288]{0:T(1024)(128)(2,1)})) %all-reduce.25.cloned.1.call-update) | async-done | bytes 3342352 | tf_op jit(solution)/shard_map/psum | solution.py:679
  (811 shorter events, 175.0 us)
Async XLA Ops:
  7.3 7.2 copy-start.184
  7.4 7.8 copy-start.185
  7.4 8.4 copy-start.255
  7.4 8.6 copy-start.256
  7.4 8.8 copy-start.257
  7.4 9.0 copy-start.258
  7.4 9.3 copy-start.259
  7.4 9.5 copy-start.260
  7.4 9.7 copy-start.261
  7.4 9.9 copy-start.262
  7.4 160.0 %all-gather.6.cloned.1.call-start = ((), (), s32[]{:S(2)}) async-start(), calls=%async_computation.3 | async-start | bytes 11206656 | tf_op jit(solution)/shard_map/all_gather | solution.py:68
  19.0 7.1 copy-start.11
  20.1 273.2 %all-gather.8.cloned.1.call-start = ((), (), s32[]{:S(2)}) async-start(), calls=%async_computation.4 | async-start | bytes 9437184 | tf_op jit(solution)/shard_map/all_gather | solution.py:81
  21.4 7.8 collective-permute-start
  26.0 292.2 %all-gather.10.cloned.1.call-start = ((), (), s32[]{:S(2)}) async-start(), calls=%async_computation.5 | async-start | bytes 2621440 | tf_op jit(solution)/shard_map/all_gather | solution.py:35
  26.2 189.4 %copy-start.133 = (f32[64,64]{0,1:T(8,128)}, f32[64,64]{0,1:T(8,128)S(1)}, u32[]{:S(2)}) copy-start(f32[64,64]{0,1:T(8,128)S(1)} %fusion.214) | copy-start | bytes 49156
  26.3 144.1 %copy-start.195 = (f32[128]{0:T(128)}, f32[128]{0:T(128)S(1)}, u32[]{:S(2)}) copy-start(f32[128]{0:T(128)S(1)} %broadcast_multiply_fusion.6) | copy-start | bytes 1540
  27.3 143.1 %copy-start.220 = (f32[128]{0:T(128)}, f32[128]{0:T(128)S(1)}, u32[]{:S(2)}) copy-start(f32[128]{0:T(128)S(1)} %fusion.234) | copy-start | bytes 1540
  32.3 137.3 %copy-start.225 = (f32[128]{0:T(128)}, f32[128]{0:T(128)S(1)}, u32[]{:S(2)}) copy-start(f32[128]{0:T(128)S(1)} %get-tuple-element.198) | copy-start | bytes 1540
  169.6 9.3 copy-start.31
  170.4 8.5 copy-start.147
  171.2 5.7 collective-permute-start.1
  174.0 7.6 copy-start.162
  174.0 7.6 copy-start.165
  174.0 7.6 copy-start.168
  174.3 7.4 copy-start.63
  174.4 8.0 copy-start.126
  176.9 13.8 %copy-start.67 = (bf16[1024,64]{1,0:T(8,128)(2,1)}, bf16[1024,64]{1,0:T(8,128)(2,1)S(1)}, u32[]{:S(2)}) copy-start(bf16[1024,64]{1,0:T(8,128)(2,1)S(1)} %reshape.651) | copy-start | bytes 393220
  181.7 9.1 copy-start.76
  181.7 12.6 %copy-start.29 = (bf16[128,1024]{1,0:T(8,128)(2,1)}, bf16[128,1024]{1,0:T(8,128)(2,1)S(1)}, u32[]{:S(2)}) copy-start(bf16[128,1024]{1,0:T(8,128)(2,1)S(1)} %get-tuple-element.144) | copy-start | bytes 786436
  187.0 119.6 %copy-start.3 = (f32[128,1024]{0,1:T(8,128)}, f32[128,1024]{0,1:T(8,128)S(1)}, u32[]{:S(2)}) copy-start(f32[128,1024]{0,1:T(8,128)S(1)} %copy.213) | copy-start | bytes 1572868
  190.5 121.1 %copy-start.12 = (f32[128,1024]{0,1:T(8,128)}, f32[128,1024]{0,1:T(8,128)S(1)}, u32[]{:S(2)}) copy-start(f32[128,1024]{0,1:T(8,128)S(1)} %copy.212) | copy-start | bytes 1572868
  190.7 9.5 copy-start.15
  200.2 16.3 %copy-start.137 = (f32[16,64]{1,0:T(8,128)}, f32[16,64]{1,0:T(8,128)S(1)}, u32[]{:S(2)}) copy-start(f32[16,64]{1,0:T(8,128)S(1)} %get-tuple-element.73) | copy-start | bytes 12292
  201.8 13.1 %copy-start.25 = (f32[128,16,64]{0,2,1:T(8,128)}, f32[128,16,64]{0,2,1:T(8,128)S(1)}, u32[]{:S(2)}) copy-start(f32[128,16,64]{0,2,1:T(8,128)S(1)} %get-tuple-element.136) | copy-start | bytes 1572868
  203.8 8.5 copy-start
  214.9 94.4 %copy-start.1 = (f32[16,128,128]{2,1,0:T(8,128)}, f32[16,128,128]{2,1,0:T(8,128)S(1)}, u32[]{:S(2)}) copy-start(f32[16,128,128]{2,1,0:T(8,128)S(1)} %fusion.52) | copy-start | bytes 3145732
  297.3 148.4 %all-gather.12.cloned.1.call-start = ((), (), s32[]{:S(2)}) async-start(), calls=%async_computation.6 | async-start | bytes 9437184 | tf_op jit(solution)/shard_map/all_gather | solution.py:81
  299.7 296.8 %reduce-scatter.6.cloned.1.call-start = ((), (), s32[]{:S(2)}) async-start(), calls=%async_computation.7 | async-start | bytes 9437184 | tf_op jit(solution)/shard_map/reduce_scatter | solution.py:86
  312.7 10.4 %copy-start.34 = (f32[16,128,64]{1,2,0:T(8,128)}, f32[16,128,64]{1,2,0:T(8,128)S(1)}, u32[]{:S(2)}) copy-start(f32[16,128,64]{1,2,0:T(8,128)S(1)} %slice_subtract_fusion.1) | copy-start | bytes 1572868
  334.3 3.0 collective-permute-start.2
  349.3 399.1 %reduce-scatter.8.cloned.1.call-start = ((), (), s32[]{:S(2)}) async-start(), calls=%async_computation.8 | async-start | bytes 9437184 | tf_op jit(solution)/shard_map/reduce_scatter | solution.py:86
  452.2 11.1 %copy-start.61 = (bf16[128,1024]{1,0:T(8,128)(2,1)S(1)}, bf16[128,1024]{1,0:T(8,128)(2,1)}, u32[]{:S(2)}) copy-start(bf16[128,1024]{1,0:T(8,128)(2,1)} %copy-done.60) | copy-start | bytes 786436
  462.0 9.0 collective-permute-start.3
  470.9 460.6 %reduce-scatter.10.cloned.1.call-start = ((), (), s32[]{:S(2)}) async-start(), calls=%async_computation.9 | async-start | bytes 11206656
  526.1 7.6 copy-start.153
  547.8 7.8 copy-start.156
  547.8 7.8 copy-start.200
  547.8 7.8 copy-start.227
  562.5 38.1 %copy-start.129 = (bf16[64,1024]{1,0:T(8,128)(2,1)S(1)}, bf16[64,1024]{1,0:T(8,128)(2,1)}, u32[]{:S(2)}) copy-start(bf16[64,1024]{1,0:T(8,128)(2,1)} %reshape.652) | copy-start | bytes 393220
  598.5 7.0 copy-start.99
  598.5 7.0 copy-start.100
  598.6 7.0 copy-start.159
  632.6 7.8 copy-start.194
  633.2 31.0 %collective-permute-start.4 = (f32[1,1024]{1,0:T(1,128)}, f32[1,1024]{1,0:T(1,128)}, u32[]{:S(2)}, u32[]{:S(2)}) collective-permute-start(f32[1,1024]{1,0:T(1,128)} %split.49), channel_id=1, source_target_pairs={{1,0},{2,1},{3,2},{5,4},{6,5},{7,6},{9,8},{10,9},{11,10},{13,12},{... | collective-permute-start | bytes 12296 | tf_op jit(solution)/shard_map/ppermute | solution.py:25
  635.4 10.2 copy-start.70
  637.4 8.1 copy-start.136
  637.4 8.9 copy-start.144
  637.5 8.9 copy-start.146
  654.8 9.5 copy-start.148
  654.8 9.5 copy-start.164
  654.8 9.5 copy-start.167
  654.8 9.5 copy-start.170
  761.6 244.1 %all-reduce.25.cloned.1.call-start = ((), (), s32[]{:S(2)}) async-start(), calls=%async_computation.10 | async-start | bytes 6684672 | tf_op jit(solution)/shard_map/psum | solution.py:679
  (215 other events, 701.6 us)
Sparse Core Ops, SparseCore 0:
  20.2 147.1 all-gather.5
  170.1 123.1 all-gather.7
  297.4 20.7 all-gather.9
  320.8 124.9 all-gather.11
  449.2 147.1 reduce-scatter.5
  600.4 148.0 reduce-scatter.7
  761.8 169.6 reduce-scatter.9
  934.6 71.1 all-reduce.24
